TPU v7x, 32 devices: a whole 2x2x4 slice. The times are simulated.
32 devices in a mesh: front: 8 (over z, x), rhs: 4 (over y, core).
Axes of the slice: x: 2, y: 2, z: 4, core: 2. Of those that a mesh axis runs over, the one named last changes fastest.
Arguments:
- signs: int32 [128, 512], P('rhs'), may hold values from -1 to 1, as said below
- sources: bfloat16 [512, 16384], P(None, 'front'), may hold values from -0.25 to 0.25
- dinv: float32 [64, 256, 256], P('front')
- u_fac: float32 [64, 256, 32], P('front')
- v_fac: float32 [64, 256, 32], P('front')
- ranks: int32 [64], P('front'), may hold values from 8 to 32
- dobs: bfloat16 [128, 16384], P('rhs', 'front'), may hold values from -6 to 6
- cellmap: int32 [16384], replicated, may hold values from 0 to 65535, as said below
Outputs:
- wavefield: float32 [128, 16384], P('rhs', 'front')
- adjoint_field: float32 [128, 16384], P('rhs', 'front')
- gradient: float32 [65536], P('front')
Inputs may be any that keep to these rules, and one draw needn't show every extreme that they name: `signs`: each entry is -1 or 1. `cellmap`: model cell m belongs to owner m // 8192; among the cells k * 8 * 256 to (k + 1) * 8 * 256 - 1, for each k, at most 512 have one owner, and in every such block some owner has exactly 512.
All inputs are finite; a program needn't handle non-finite values.
Results may differ from a plain program's by a relative error of at most 0.0003.
Values sent between devices are 32-bit elements; how exact they have to be, the bound alone decides.
No kernel may reach another device: no remote copies, remote signals or barrier semaphores. Data moves between devices by JAX's collectives and lax.ppermute only.
A program may use at most 64 MiB of HBM per device.

v0:
```python
import jax
import jax.numpy as jnp
from jax import lax
from jax.sharding import PartitionSpec as P

MC_DEV = 8192


HIGHEST = lax.Precision.HIGHEST


def from_behind(array, axis, by):
    length = lax.axis_size(axis)
    pairs = [(i, i + by) for i in range(length) if 0 <= i + by < length]
    return lax.ppermute(array, axis, pairs)


def forward_step(state, inputs):
    source, inverse, left, right_next = inputs
    field = jnp.dot(
        source - jnp.dot(state, left.T, precision=HIGHEST), inverse.T, precision=HIGHEST
    )
    return (jnp.dot(field, right_next, precision=HIGHEST), field)


def adjoint_step(state, inputs):
    source, inverse, left, right_next = inputs
    field = jnp.dot(
        source - jnp.dot(state, right_next.T, precision=HIGHEST), inverse, precision=HIGHEST
    )
    return (jnp.dot(field, left, precision=HIGHEST), field)


def body(signs, sources, dinv, u_fac, v_fac, ranks, dobs, cellmap):
    shots = signs.shape[0]
    blocks, width, rank_max = u_fac.shape
    fronts = lax.axis_size("front")
    encoded = jnp.dot(signs.astype(jnp.bfloat16), sources, preferred_element_type=jnp.float32)
    live = (jnp.arange(rank_max)[None, :] < ranks[:, None]).astype(jnp.float32)
    left_live = u_fac * live[:, None, :]
    right_live = v_fac * live[:, None, :]
    following = from_behind(right_live[0], "front", -1)
    right_next = jnp.concatenate([right_live[1:], following[None]], axis=0)
    unit = jnp.eye(rank_max, dtype=jnp.float32)
    zero_state = jnp.zeros((shots, rank_max), jnp.float32)
    start = jnp.concatenate([zero_state, unit], axis=0)
    padding = jnp.zeros((blocks, rank_max, width), jnp.float32)
    source_blocks = encoded.reshape(shots, blocks, width).transpose(1, 0, 2)
    extended = jnp.concatenate([source_blocks, padding], axis=1)
    final, fields = lax.scan(forward_step, start, (extended, dinv, left_live, right_next))
    forward_map = final[shots:]
    forward_offset = final[:shots]

    def relay_forward(position, state):
        moved = jnp.dot(state, forward_map, precision=HIGHEST) + forward_offset
        return from_behind(moved, "front", 1)

    incoming = lax.fori_loop(0, fronts - 1, relay_forward, zero_state)
    wave = fields[:, :shots] + jnp.einsum(
        "sr,krc->ksc", incoming, fields[:, shots:], precision=HIGHEST
    )
    residual = wave - dobs.astype(jnp.float32).reshape(shots, blocks, width).transpose(1, 0, 2)
    extended_back = jnp.concatenate([residual, padding], axis=1)
    back_final, back_fields = lax.scan(
        adjoint_step, start, (extended_back, dinv, left_live, right_next), reverse=True
    )
    backward_map = back_final[shots:]
    backward_offset = back_final[:shots]

    def relay_backward(position, state):
        moved = jnp.dot(state, backward_map, precision=HIGHEST) + backward_offset
        return from_behind(moved, "front", -1)

    arriving = lax.fori_loop(0, fronts - 1, relay_backward, zero_state)
    adjoint = back_fields[:, :shots] + jnp.einsum(
        "sr,krc->ksc", arriving, back_fields[:, shots:], precision=HIGHEST
    )
    image = (jnp.sum(wave * adjoint, axis=1) / (shots * lax.axis_size("rhs"))).reshape(
        blocks * width
    )
    cell_rows = blocks * width
    my_front = lax.axis_index("front")
    own_map = lax.dynamic_slice_in_dim(cellmap, my_front * cell_rows, cell_rows)
    model_cells = MC_DEV * fronts
    summed = lax.psum(image, "rhs")
    dense = jnp.zeros((model_cells,), jnp.float32).at[own_map].add(summed)
    gradient = lax.psum_scatter(dense, "front", scatter_dimension=0, tiled=True)
    wavefield = wave.transpose(1, 0, 2).reshape(shots, blocks * width)
    adjoint_field = adjoint.transpose(1, 0, 2).reshape(shots, blocks * width)
    return (wavefield, adjoint_field, gradient)


def solution(mesh):
    in_specs = (
        P("rhs", None),
        P(None, "front"),
        P("front", None, None),
        P("front", None, None),
        P("front", None, None),
        P("front"),
        P("rhs", "front"),
        P(),
    )
    out_specs = (P("rhs", "front"), P("rhs", "front"), P("front"))
    return jax.shard_map(body, mesh=mesh, in_specs=in_specs, out_specs=out_specs, check_vma=False)
```

profile of v0, /device:TPU:0, one launch (start us, length us, event | category | flops | bytes accessed | tf_op | source)
XLA Modules:
  0.0 280.9 jit_solution(9179130558951455886)
XLA Ops:
  8.1 1.8 broadcast_multiply_fusion
  21.0 34.8 %while.48 = (s32[]{:T(128)}, f32[64,32]{0,1:T(8,128)S(1)}, f32[8,64,256]{2,1,0:T(8,128)}, f32[8,64,256]{2,1,0:T(8,128)}, f32[8,256,32]{2,1,0:T(8,128)S(1)}, /*in...) while((s32[]{:T(128)}, f32[64,32]{0,1:T(8,128)S(1)}, f32[8,64,256]{2,1,0:T(8,128)}, ...), condition=%wide.region_1.2_spmd, body=%wide.region_0.1_spmd.sunk | while | flops 62930944 | bytes 944725 | solution.py:50
  22.1 1.9 bitcast_dynamic-update-slice_fusion.4
  26.4 1.9 bitcast_dynamic-update-slice_fusion.4
  30.8 1.9 bitcast_dynamic-update-slice_fusion.4
  35.2 1.9 bitcast_dynamic-update-slice_fusion.4
  39.5 1.9 bitcast_dynamic-update-slice_fusion.4
  43.9 1.9 bitcast_dynamic-update-slice_fusion.4
  48.2 1.9 bitcast_dynamic-update-slice_fusion.4
  52.6 1.9 bitcast_dynamic-update-slice_fusion.4
  55.9 46.8 %while.49 = (s32[]{:T(128)}, f32[32,32]{1,0:T(8,128)S(1)}, f32[32,32]{1,0:T(8,128)S(1)}, f32[32,32]{1,0:T(8,128)S(1)}, s32[]{:T(128)}) while((s32[]{:T(128)}, f32[32,32]{1,0:T(8,128)S(1)}, f32[32,32]{1,0:T(8,128)S(1)}, f32[32,32]{1,0:T(8,128)S(1)}, s32[]{:T(128)}) %tuple.93), condition=%wide.region_3.4_spmd, body=%wide.region_2.3_spmd.sunk | while | flops 394242 | bytes 32869 | solution.py:58
  56.0 5.5 %collective-permute-start = (f32[32,32]{1,0:T(8,128)S(1)}, f32[32,32]{1,0:T(8,128)S(1)}, u32[]{:S(2)}, u32[]{:S(2)}) collective-permute-start(f32[32,32]{1,0:T(8,128)S(1)} %convolution_add_fusion.4), channel_id=1, source_target_pairs={{0,4},{4,8},{8,12},{12,16},{16,20},{20,24},{24,28},{1,5},{5,9},{9,... | collective-permute-start | bytes 12296 | tf_op jit(solution)/shard_map/while/body/eval_jaxpr/ppermute | solution.py:15
  63.1 4.8 %collective-permute-start = (f32[32,32]{1,0:T(8,128)S(1)}, f32[32,32]{1,0:T(8,128)S(1)}, u32[]{:S(2)}, u32[]{:S(2)}) collective-permute-start(f32[32,32]{1,0:T(8,128)S(1)} %convolution_add_fusion.4), channel_id=1, source_target_pairs={{0,4},{4,8},{8,12},{12,16},{16,20},{20,24},{24,28},{1,5},{5,9},{9,... | collective-permute-start | bytes 12296 | tf_op jit(solution)/shard_map/while/body/eval_jaxpr/ppermute | solution.py:15
  69.5 5.1 %collective-permute-start = (f32[32,32]{1,0:T(8,128)S(1)}, f32[32,32]{1,0:T(8,128)S(1)}, u32[]{:S(2)}, u32[]{:S(2)}) collective-permute-start(f32[32,32]{1,0:T(8,128)S(1)} %convolution_add_fusion.4), channel_id=1, source_target_pairs={{0,4},{4,8},{8,12},{12,16},{16,20},{20,24},{24,28},{1,5},{5,9},{9,... | collective-permute-start | bytes 12296 | tf_op jit(solution)/shard_map/while/body/eval_jaxpr/ppermute | solution.py:15
  76.2 5.1 %collective-permute-start = (f32[32,32]{1,0:T(8,128)S(1)}, f32[32,32]{1,0:T(8,128)S(1)}, u32[]{:S(2)}, u32[]{:S(2)}) collective-permute-start(f32[32,32]{1,0:T(8,128)S(1)} %convolution_add_fusion.4), channel_id=1, source_target_pairs={{0,4},{4,8},{8,12},{12,16},{16,20},{20,24},{24,28},{1,5},{5,9},{9,... | collective-permute-start | bytes 12296 | tf_op jit(solution)/shard_map/while/body/eval_jaxpr/ppermute | solution.py:15
  82.8 5.1 %collective-permute-start = (f32[32,32]{1,0:T(8,128)S(1)}, f32[32,32]{1,0:T(8,128)S(1)}, u32[]{:S(2)}, u32[]{:S(2)}) collective-permute-start(f32[32,32]{1,0:T(8,128)S(1)} %convolution_add_fusion.4), channel_id=1, source_target_pairs={{0,4},{4,8},{8,12},{12,16},{16,20},{20,24},{24,28},{1,5},{5,9},{9,... | collective-permute-start | bytes 12296 | tf_op jit(solution)/shard_map/while/body/eval_jaxpr/ppermute | solution.py:15
  89.5 5.1 %collective-permute-start = (f32[32,32]{1,0:T(8,128)S(1)}, f32[32,32]{1,0:T(8,128)S(1)}, u32[]{:S(2)}, u32[]{:S(2)}) collective-permute-start(f32[32,32]{1,0:T(8,128)S(1)} %convolution_add_fusion.4), channel_id=1, source_target_pairs={{0,4},{4,8},{8,12},{12,16},{16,20},{20,24},{24,28},{1,5},{5,9},{9,... | collective-permute-start | bytes 12296 | tf_op jit(solution)/shard_map/while/body/eval_jaxpr/ppermute | solution.py:15
  96.2 5.1 %collective-permute-start = (f32[32,32]{1,0:T(8,128)S(1)}, f32[32,32]{1,0:T(8,128)S(1)}, u32[]{:S(2)}, u32[]{:S(2)}) collective-permute-start(f32[32,32]{1,0:T(8,128)S(1)} %convolution_add_fusion.4), channel_id=1, source_target_pairs={{0,4},{4,8},{8,12},{12,16},{16,20},{20,24},{24,28},{1,5},{5,9},{9,... | collective-permute-start | bytes 12296 | tf_op jit(solution)/shard_map/while/body/eval_jaxpr/ppermute | solution.py:15
  105.9 27.2 %while.50 = (s32[]{:T(128)}, f32[64,32]{0,1:T(8,128)S(1)}, f32[8,64,256]{2,1,0:T(8,128)}, f32[8,64,256]{2,1,0:T(8,128)}, f32[8,256,32]{2,1,0:T(8,128)}, /*index=...) while((s32[]{:T(128)}, f32[64,32]{0,1:T(8,128)S(1)}, f32[8,64,256]{2,1,0:T(8,128)}, ...), condition=%wide.region_5.6_spmd, body=%wide.region_4.5_spmd.sunk | while | flops 62930944 | bytes 936045 | solution.py:64
  113.9 1.8 bitcast_dynamic-update-slice_fusion.5
  124.1 1.8 bitcast_dynamic-update-slice_fusion.5
  133.2 47.3 %while.51 = (s32[]{:T(128)}, f32[32,32]{1,0:T(8,128)S(1)}, f32[32,32]{1,0:T(8,128)S(1)}, f32[32,32]{1,0:T(8,128)S(1)}, s32[]{:T(128)}) while((s32[]{:T(128)}, f32[32,32]{1,0:T(8,128)S(1)}, f32[32,32]{1,0:T(8,128)S(1)}, f32[32,32]{1,0:T(8,128)S(1)}, s32[]{:T(128)}) %tuple.99), condition=%wide.region_7.8_spmd, body=%wide.region_6.7_spmd.sunk | while | flops 394242 | bytes 32869 | solution.py:74
  134.7 5.5 %collective-permute-done.1 = f32[32,32]{1,0:T(8,128)S(1)} collective-permute-done((f32[32,32]{1,0:T(8,128)S(1)}, f32[32,32]{1,0:T(8,128)S(1)}, u32[]{:S(2)}, u32[]{:S(2)}) %collective-permute-start.1) | collective-permute-done | bytes 4128 | tf_op jit(solution)/shard_map/while/body/eval_jaxpr/ppermute | solution.py:15
  141.6 5.5 %collective-permute-done.1 = f32[32,32]{1,0:T(8,128)S(1)} collective-permute-done((f32[32,32]{1,0:T(8,128)S(1)}, f32[32,32]{1,0:T(8,128)S(1)}, u32[]{:S(2)}, u32[]{:S(2)}) %collective-permute-start.1) | collective-permute-done | bytes 4128 | tf_op jit(solution)/shard_map/while/body/eval_jaxpr/ppermute | solution.py:15
  148.6 5.3 %collective-permute-done.1 = f32[32,32]{1,0:T(8,128)S(1)} collective-permute-done((f32[32,32]{1,0:T(8,128)S(1)}, f32[32,32]{1,0:T(8,128)S(1)}, u32[]{:S(2)}, u32[]{:S(2)}) %collective-permute-start.1) | collective-permute-done | bytes 4128 | tf_op jit(solution)/shard_map/while/body/eval_jaxpr/ppermute | solution.py:15
  155.3 5.2 %collective-permute-done.1 = f32[32,32]{1,0:T(8,128)S(1)} collective-permute-done((f32[32,32]{1,0:T(8,128)S(1)}, f32[32,32]{1,0:T(8,128)S(1)}, u32[]{:S(2)}, u32[]{:S(2)}) %collective-permute-start.1) | collective-permute-done | bytes 4128 | tf_op jit(solution)/shard_map/while/body/eval_jaxpr/ppermute | solution.py:15
  161.9 5.2 %collective-permute-done.1 = f32[32,32]{1,0:T(8,128)S(1)} collective-permute-done((f32[32,32]{1,0:T(8,128)S(1)}, f32[32,32]{1,0:T(8,128)S(1)}, u32[]{:S(2)}, u32[]{:S(2)}) %collective-permute-start.1) | collective-permute-done | bytes 4128 | tf_op jit(solution)/shard_map/while/body/eval_jaxpr/ppermute | solution.py:15
  168.6 5.2 %collective-permute-done.1 = f32[32,32]{1,0:T(8,128)S(1)} collective-permute-done((f32[32,32]{1,0:T(8,128)S(1)}, f32[32,32]{1,0:T(8,128)S(1)}, u32[]{:S(2)}, u32[]{:S(2)}) %collective-permute-start.1) | collective-permute-done | bytes 4128 | tf_op jit(solution)/shard_map/while/body/eval_jaxpr/ppermute | solution.py:15
  175.3 5.2 %collective-permute-done.1 = f32[32,32]{1,0:T(8,128)S(1)} collective-permute-done((f32[32,32]{1,0:T(8,128)S(1)}, f32[32,32]{1,0:T(8,128)S(1)}, u32[]{:S(2)}, u32[]{:S(2)}) %collective-permute-start.1) | collective-permute-done | bytes 4128 | tf_op jit(solution)/shard_map/while/body/eval_jaxpr/ppermute | solution.py:15
  182.0 5.8 %psum.7 = f32[2048]{0:T(1024)S(1)} all-reduce(f32[2048]{0:T(1024)S(1)} %bitcast.148), channel_id=1, replica_groups=mesh['front'=8,'rhs'=4] {'rhs'}, use_global_device_ids=true, to_apply=%region_9.10 | all-reduce | flops 2048 | bytes 16384 | tf_op jit(solution)/shard_map/psum | solution.py:85
  187.7 11.9 %scatter_custom_fusion = f32[65536]{0:T(1024)} fusion(s32[2048]{0:T(1024)S(1)} %compare_select_fusion, f32[2048]{0:T(1024)S(1)} %psum.7, f32[]{:T(128)} %constant.79.clone.1), kind=kCustom, calls=%fused_computation.42 | custom fusion | flops 2048 | bytes 262148 | tf_op jit(solution)/shard_map/scatter-add | solution.py:86
  202.4 70.3 %all-reduce.6.cloned.1.call-done = f32[65536]{0:T(1024)} async-done(((f32[65536]{0:T(1024)}), f32[65536]{0:T(1024)}) %all-reduce.6.cloned.1.call-update) | async-done | bytes 262160
  (105 shorter events, 83.3 us)
Async XLA Ops:
  7.2 4.1 %copy-start = (bf16[512,2048]{1,0:T(8,128)(2,1)S(1)}, bf16[512,2048]{1,0:T(8,128)(2,1)}, u32[]{:S(2)}) copy-start(bf16[512,2048]{1,0:T(8,128)(2,1)} %param.17) | copy-start | bytes 6291460
  7.2 265.5 %all-reduce.6.cloned.1.call-start = ((), (), s32[]{:S(2)}) async-start(), calls=%async_computation | async-start | bytes 524288
  9.9 7.9 %collective-permute-start.2 = (f32[256,32]{0,1:T(8,128)S(1)}, f32[256,32]{0,1:T(8,128)S(1)}, u32[]{:S(2)}, u32[]{:S(2)}) collective-permute-start(f32[256,32]{0,1:T(8,128)S(1)} %slice_bitcast_fusion), channel_id=1, source_target_pairs={{4,0},{8,4},{12,8},{16,12},{20,16},{24,20},{28,24},{5,1},{9,5},{13... | collective-permute-start | bytes 98312 | tf_op jit(solution)/shard_map/ppermute | solution.py:15
  56.0 6.9 %collective-permute-start = (f32[32,32]{1,0:T(8,128)S(1)}, f32[32,32]{1,0:T(8,128)S(1)}, u32[]{:S(2)}, u32[]{:S(2)}) collective-permute-start(f32[32,32]{1,0:T(8,128)S(1)} %convolution_add_fusion.4), channel_id=1, source_target_pairs={{0,4},{4,8},{8,12},{12,16},{16,20},{20,24},{24,28},{1,5},{5,9},{9,... | collective-permute-start | bytes 12296 | tf_op jit(solution)/shard_map/while/body/eval_jaxpr/ppermute | solution.py:15
  63.1 6.2 %collective-permute-start = (f32[32,32]{1,0:T(8,128)S(1)}, f32[32,32]{1,0:T(8,128)S(1)}, u32[]{:S(2)}, u32[]{:S(2)}) collective-permute-start(f32[32,32]{1,0:T(8,128)S(1)} %convolution_add_fusion.4), channel_id=1, source_target_pairs={{0,4},{4,8},{8,12},{12,16},{16,20},{20,24},{24,28},{1,5},{5,9},{9,... | collective-permute-start | bytes 12296 | tf_op jit(solution)/shard_map/while/body/eval_jaxpr/ppermute | solution.py:15
  69.5 6.5 %collective-permute-start = (f32[32,32]{1,0:T(8,128)S(1)}, f32[32,32]{1,0:T(8,128)S(1)}, u32[]{:S(2)}, u32[]{:S(2)}) collective-permute-start(f32[32,32]{1,0:T(8,128)S(1)} %convolution_add_fusion.4), channel_id=1, source_target_pairs={{0,4},{4,8},{8,12},{12,16},{16,20},{20,24},{24,28},{1,5},{5,9},{9,... | collective-permute-start | bytes 12296 | tf_op jit(solution)/shard_map/while/body/eval_jaxpr/ppermute | solution.py:15
  76.2 6.5 %collective-permute-start = (f32[32,32]{1,0:T(8,128)S(1)}, f32[32,32]{1,0:T(8,128)S(1)}, u32[]{:S(2)}, u32[]{:S(2)}) collective-permute-start(f32[32,32]{1,0:T(8,128)S(1)} %convolution_add_fusion.4), channel_id=1, source_target_pairs={{0,4},{4,8},{8,12},{12,16},{16,20},{20,24},{24,28},{1,5},{5,9},{9,... | collective-permute-start | bytes 12296 | tf_op jit(solution)/shard_map/while/body/eval_jaxpr/ppermute | solution.py:15
  82.8 6.5 %collective-permute-start = (f32[32,32]{1,0:T(8,128)S(1)}, f32[32,32]{1,0:T(8,128)S(1)}, u32[]{:S(2)}, u32[]{:S(2)}) collective-permute-start(f32[32,32]{1,0:T(8,128)S(1)} %convolution_add_fusion.4), channel_id=1, source_target_pairs={{0,4},{4,8},{8,12},{12,16},{16,20},{20,24},{24,28},{1,5},{5,9},{9,... | collective-permute-start | bytes 12296 | tf_op jit(solution)/shard_map/while/body/eval_jaxpr/ppermute | solution.py:15
  89.5 6.5 %collective-permute-start = (f32[32,32]{1,0:T(8,128)S(1)}, f32[32,32]{1,0:T(8,128)S(1)}, u32[]{:S(2)}, u32[]{:S(2)}) collective-permute-start(f32[32,32]{1,0:T(8,128)S(1)} %convolution_add_fusion.4), channel_id=1, source_target_pairs={{0,4},{4,8},{8,12},{12,16},{16,20},{20,24},{24,28},{1,5},{5,9},{9,... | collective-permute-start | bytes 12296 | tf_op jit(solution)/shard_map/while/body/eval_jaxpr/ppermute | solution.py:15
  96.2 6.5 %collective-permute-start = (f32[32,32]{1,0:T(8,128)S(1)}, f32[32,32]{1,0:T(8,128)S(1)}, u32[]{:S(2)}, u32[]{:S(2)}) collective-permute-start(f32[32,32]{1,0:T(8,128)S(1)} %convolution_add_fusion.4), channel_id=1, source_target_pairs={{0,4},{4,8},{8,12},{12,16},{16,20},{20,24},{24,28},{1,5},{5,9},{9,... | collective-permute-start | bytes 12296 | tf_op jit(solution)/shard_map/while/body/eval_jaxpr/ppermute | solution.py:15
  105.9 93.8 %copy-start.1 = (u32[32]{0:T(128)S(1)}, u32[32]{0:T(128)}, u32[]{:S(2)}) copy-start(u32[32]{0:T(128)} %constant.94) | copy-start | bytes 388
  133.4 6.8 %collective-permute-start.1 = (f32[32,32]{1,0:T(8,128)S(1)}, f32[32,32]{1,0:T(8,128)S(1)}, u32[]{:S(2)}, u32[]{:S(2)}) collective-permute-start(f32[32,32]{1,0:T(8,128)S(1)} %convolution_add_fusion.5), channel_id=1, source_target_pairs={{4,0},{8,4},{12,8},{16,12},{20,16},{24,20},{28,24},{5,1},{9,5},{13... | collective-permute-start | bytes 12296 | tf_op jit(solution)/shard_map/while/body/eval_jaxpr/ppermute | solution.py:15
  140.3 6.8 %collective-permute-start.1 = (f32[32,32]{1,0:T(8,128)S(1)}, f32[32,32]{1,0:T(8,128)S(1)}, u32[]{:S(2)}, u32[]{:S(2)}) collective-permute-start(f32[32,32]{1,0:T(8,128)S(1)} %convolution_add_fusion.5), channel_id=1, source_target_pairs={{4,0},{8,4},{12,8},{16,12},{20,16},{24,20},{28,24},{5,1},{9,5},{13... | collective-permute-start | bytes 12296 | tf_op jit(solution)/shard_map/while/body/eval_jaxpr/ppermute | solution.py:15
  147.3 6.6 %collective-permute-start.1 = (f32[32,32]{1,0:T(8,128)S(1)}, f32[32,32]{1,0:T(8,128)S(1)}, u32[]{:S(2)}, u32[]{:S(2)}) collective-permute-start(f32[32,32]{1,0:T(8,128)S(1)} %convolution_add_fusion.5), channel_id=1, source_target_pairs={{4,0},{8,4},{12,8},{16,12},{20,16},{24,20},{28,24},{5,1},{9,5},{13... | collective-permute-start | bytes 12296 | tf_op jit(solution)/shard_map/while/body/eval_jaxpr/ppermute | solution.py:15
  154.0 6.5 %collective-permute-start.1 = (f32[32,32]{1,0:T(8,128)S(1)}, f32[32,32]{1,0:T(8,128)S(1)}, u32[]{:S(2)}, u32[]{:S(2)}) collective-permute-start(f32[32,32]{1,0:T(8,128)S(1)} %convolution_add_fusion.5), channel_id=1, source_target_pairs={{4,0},{8,4},{12,8},{16,12},{20,16},{24,20},{28,24},{5,1},{9,5},{13... | collective-permute-start | bytes 12296 | tf_op jit(solution)/shard_map/while/body/eval_jaxpr/ppermute | solution.py:15
  160.6 6.5 %collective-permute-start.1 = (f32[32,32]{1,0:T(8,128)S(1)}, f32[32,32]{1,0:T(8,128)S(1)}, u32[]{:S(2)}, u32[]{:S(2)}) collective-permute-start(f32[32,32]{1,0:T(8,128)S(1)} %convolution_add_fusion.5), channel_id=1, source_target_pairs={{4,0},{8,4},{12,8},{16,12},{20,16},{24,20},{28,24},{5,1},{9,5},{13... | collective-permute-start | bytes 12296 | tf_op jit(solution)/shard_map/while/body/eval_jaxpr/ppermute | solution.py:15
  167.3 6.5 %collective-permute-start.1 = (f32[32,32]{1,0:T(8,128)S(1)}, f32[32,32]{1,0:T(8,128)S(1)}, u32[]{:S(2)}, u32[]{:S(2)}) collective-permute-start(f32[32,32]{1,0:T(8,128)S(1)} %convolution_add_fusion.5), channel_id=1, source_target_pairs={{4,0},{8,4},{12,8},{16,12},{20,16},{24,20},{28,24},{5,1},{9,5},{13... | collective-permute-start | bytes 12296 | tf_op jit(solution)/shard_map/while/body/eval_jaxpr/ppermute | solution.py:15
  174.0 6.5 %collective-permute-start.1 = (f32[32,32]{1,0:T(8,128)S(1)}, f32[32,32]{1,0:T(8,128)S(1)}, u32[]{:S(2)}, u32[]{:S(2)}) collective-permute-start(f32[32,32]{1,0:T(8,128)S(1)} %convolution_add_fusion.5), channel_id=1, source_target_pairs={{4,0},{8,4},{12,8},{16,12},{20,16},{24,20},{28,24},{5,1},{9,5},{13... | collective-permute-start | bytes 12296 | tf_op jit(solution)/shard_map/while/body/eval_jaxpr/ppermute | solution.py:15
Sparse Core Ops, SparseCore 0:
  199.8 72.8 all-reduce.5
where the time goes:
time: 283 us; the launch traced here: 281 us
  waiting for transfers between devices  117 us (41%)
  matrix products  67.7 us (24%)
  starting transfers between devices  46.2 us (16%)
  other arithmetic  18 us (6%)
  between operations  14.8 us (5%)
  local copies, waits for them, and re-layouts  10.3 us (4%)
  blocking collectives  5.77 us (2%)
    unnamed x2, waiting for transfers between devices  70.3 us
    ppermute x15, waiting for transfers between devices, from_behind(): return lax.ppermute(array, axis, pairs)  47.1 us
    ppermute x15, starting transfers between devices, from_behind(): return lax.ppermute(array, axis, pairs)  46.1 us
    dot_general x8, matrix products, forward_step(): jnp.dot(source - jnp.dot(state, left.T, precision=HIGHEST), inverse.T, pr...  15.6 us
    dot_general x8, matrix products, adjoint_step(): jnp.dot(source - jnp.dot(state, right_next.T, precision=HIGHEST), inverse...  14.6 us
    scatter-add x1, other arithmetic, body(): dense = jnp.zeros((model_cells,), jnp.float32).at[own_map].add(summed)  11.9 us
    dot_general x8, matrix products, forward_step(): return (jnp.dot(field, right_next, precision=HIGHEST), field)  9.91 us
    dot_general x8, matrix products, adjoint_step(): jnp.dot(state, right_next.T, precision=HIGHEST)  9.66 us
  transfers between devices with their start and end apart: 16, of which 15 were waited for; matrix products, arithmetic and copies ran while one was open for 3% of the time, Pallas kernels for 0%

commit v1 on v0

v1 whole, which is shorter than its diff:
```python
import functools

import jax
import jax.numpy as jnp
from jax import lax
from jax.experimental import pallas as pl
from jax.experimental.pallas import tpu as pltpu
from jax.sharding import PartitionSpec as P

MC_DEV = 8192
LANES = 128
F32 = jnp.float32
BF16 = jnp.bfloat16
HIGH = lax.Precision.HIGH
FULL = lax.Precision.HIGHEST


def nn(a, b, precision=FULL):
    return lax.dot_general(
        a, b, (((1,), (0,)), ((), ())), precision=precision, preferred_element_type=F32
    )


def nt(a, b, precision=FULL):
    return lax.dot_general(
        a, b, (((1,), (1,)), ((), ())), precision=precision, preferred_element_type=F32
    )


def two_parts(x):
    top = x.astype(BF16)
    return top, (x - top.astype(F32)).astype(BF16)


def one_hot_rows(count, index):
    return lax.broadcasted_iota(jnp.int32, (count, LANES), 0) == index


def from_behind(array, axis, by):
    length = lax.axis_size(axis)
    pairs = [(i, i + by) for i in range(length) if 0 <= i + by < length]
    return lax.ppermute(array, axis, pairs)


def prep_kernel(
    fronts, slot, front_ref, ranks_ref, signs_hbm, sources_hbm, dinv_hbm, ut_hbm, vt_hbm, dobs_hbm, map_hbm,
    wave_ref, adj_ref, ld_ref, e_ref, rd_ref, s_ref, t_ref, back_ref, place_ref, offset_ref,
    signs_v, sources_v, dinv_v, ut_v, vt_v, dobs_v, map_v, small_sem, block_sem,
):
    blocks, rank_max, width = ut_v.shape
    shots = signs_v.shape[0]
    groups = map_v.shape[0]
    start = pl.multiple_of(front_ref[0] * groups, groups)
    small = [
        pltpu.make_async_copy(map_hbm.at[pl.ds(start, groups)], map_v, small_sem.at[0]),
        pltpu.make_async_copy(signs_hbm, signs_v, small_sem.at[1]),
        pltpu.make_async_copy(ut_hbm, ut_v, small_sem.at[2]),
        pltpu.make_async_copy(vt_hbm, vt_v, small_sem.at[3]),
        pltpu.make_async_copy(dobs_hbm, dobs_v, small_sem.at[4]),
    ]
    for copy in small:
        copy.start()
    large = []
    for k in range(blocks):
        columns = pl.ds(k * width, width)
        pair = [
            pltpu.make_async_copy(sources_hbm.at[:, columns], sources_v.at[:, columns], block_sem.at[0, k]),
            pltpu.make_async_copy(dinv_hbm.at[k], dinv_v.at[k], block_sem.at[1, k]),
        ]
        for copy in pair:
            copy.start()
        large.append(pair)

    small[0].wait()
    cells = map_v[...]
    owner = cells >> (MC_DEV.bit_length() - 1)
    local = cells & (MC_DEV - 1)
    member = jnp.concatenate(
        [one_hot_rows(fronts, owner[j : j + 1]).astype(F32) for j in range(groups)], axis=0
    )
    member_b = member.astype(BF16)
    count = fronts * groups
    row = lax.broadcasted_iota(jnp.int32, (LANES, LANES), 0)
    lane = lax.broadcasted_iota(jnp.int32, (LANES, LANES), 1)
    before = (row < lane).astype(F32).astype(BF16)
    inside = nn(member_b, before, None)
    total = nn(member_b, jnp.ones((LANES, LANES), BF16), None)
    p = lax.broadcasted_iota(jnp.int32, (count, count), 0)
    q = lax.broadcasted_iota(jnp.int32, (count, count), 1)
    same = ((p & (fronts - 1)) == (q & (fronts - 1))) & (q < p)
    earlier = nn(same.astype(F32).astype(BF16), total.astype(BF16), None)
    ranked = member * (inside + earlier)
    place = jnp.concatenate(
        [jnp.sum(ranked[j * fronts : (j + 1) * fronts], axis=0, keepdims=True) for j in range(groups)], axis=0
    ).astype(jnp.int32) + owner * slot
    place_ref[...] = place
    high, low = place >> 7, place & (LANES - 1)
    out_rows = fronts * slot // LANES
    coarse = (local >> 7).astype(F32)
    fine = (local & (LANES - 1)).astype(F32)
    table, pick = [], []
    for j in range(groups):
        hit = one_hot_rows(out_rows, high[j : j + 1])
        table.append(
            jnp.concatenate(
                [jnp.where(hit, coarse[j : j + 1], 0.0), jnp.where(hit, fine[j : j + 1], 0.0)], axis=0
            ).astype(BF16)
        )
        pick.append(one_hot_rows(LANES, low[j : j + 1]).astype(F32).astype(BF16))
    found = nt(jnp.concatenate(table, axis=1), jnp.concatenate(pick, axis=1), None)
    offset_ref[...] = found[:out_rows] * float(LANES) + found[out_rows:]

    for copy in small[1:]:
        copy.wait()
    sign = signs_v[...].astype(F32).astype(BF16)
    rank_row = lax.broadcasted_iota(jnp.int32, (rank_max, width), 0)
    unit_row = lax.broadcasted_iota(jnp.int32, (rank_max, rank_max), 0)
    unit_lane = lax.broadcasted_iota(jnp.int32, (rank_max, rank_max), 1)
    unit = (unit_row == unit_lane).astype(F32)
    zero = jnp.zeros((shots, rank_max), F32)
    state = jnp.concatenate([zero, unit], axis=0)
    maps, pushes = [], []
    for k in range(blocks):
        for copy in large[k]:
            copy.wait()
        columns = slice(k * width, (k + 1) * width)
        source = nn(sign, sources_v[:, columns], None)
        inverse = dinv_v[k]
        left = jnp.where(rank_row < ranks_ref[k], ut_v[k], 0.0)
        swept = nt(jnp.concatenate([source, left], axis=0), inverse)
        wave, ld = swept[:shots], swept[shots:]
        wave_ref[:, columns] = wave
        ld_ref[k] = ld
        residual = wave - dobs_v[:, columns].astype(F32)
        both = jnp.concatenate([residual, ld], axis=0)
        if k + 1 < blocks:
            right = jnp.where(rank_row < ranks_ref[k + 1], vt_v[k + 1], 0.0)
            returned = nn(jnp.concatenate([both, right], axis=0), inverse, HIGH)
            rd_ref[k] = returned[shots + rank_max :]
        else:
            returned = nn(both, inverse, HIGH)
        adj_ref[:, columns] = returned[:shots]
        e_ref[k] = returned[shots : shots + rank_max]
        seen = nt(both, ld)
        s_ref[k] = state
        turned = nn(state, seen[shots:])
        pushes.append(jnp.concatenate([seen[:shots], jnp.zeros_like(unit)], axis=0) - turned)
        if k + 1 < blocks:
            passed = nt(swept, right)
            forward = -passed[shots:]
            maps.append(forward)
            state = nn(state, forward) + jnp.concatenate([passed[:shots], jnp.zeros_like(unit)], axis=0)

    back = jnp.concatenate([pushes[-1], unit], axis=0)
    for k in range(blocks - 2, -1, -1):
        t_ref[k] = back
        back = nt(back, maps[k]) + jnp.concatenate([pushes[k], jnp.zeros_like(unit)], axis=0)
    back_ref[...] = back[: shots + rank_max]


def send_kernel(fronts, slot, wave_ref, ld_ref, s_ref, next_ref, back_ref, offset_ref, send_ref, last_ref):
    rank_max, width = next_ref.shape
    shots = wave_ref.shape[0]
    blocks = ld_ref.shape[0]
    right = next_ref[...]
    swept = jnp.concatenate([wave_ref[:, (blocks - 1) * width :], ld_ref[blocks - 1]], axis=0)
    passed = nt(swept, right)
    forward = -passed[shots:]
    last_ref[...] = forward
    state = nn(s_ref[blocks - 1], forward)
    back = back_ref[...]
    payload = jnp.concatenate(
        [state[shots:], state[:shots] + passed[:shots], back[shots:], back[:shots]], axis=1
    )
    each = slot // LANES
    for g in range(fronts):
        send_ref[g, :rank_max] = payload
        send_ref[g, rank_max : rank_max + each] = offset_ref[g * each : (g + 1) * each]


def solve_kernel(
    fronts, slot, ranks_of_rhs, front_ref, got_ref, wave_ref, adj_ref, ld_ref, e_ref, rd_ref, s_ref, t_ref,
    next_ref, last_ref, place_ref, dinv_hbm,
    wave_out, adj_out, image_out,
    ahead_v, behind_v, dinv_v, image_v, sem,
):
    blocks, rank_max, width = ld_ref.shape
    shots = wave_ref.shape[0]
    fetch = pltpu.make_async_copy(dinv_hbm.at[blocks - 1], dinv_v, sem)
    fetch.start()
    mine = front_ref[0]
    n = rank_max

    def step_forward(g, state):
        ahead_v[g] = state
        return nn(state, got_ref[g, :n, :n]) + got_ref[g, :n, n : 2 * n]

    def step_backward(i, state):
        g = fronts - 1 - i
        behind_v[g] = state
        push = got_ref[g, :n, 3 * n : 4 * n] + nn(ahead_v[g], got_ref[g, :n, 2 * n : 3 * n])
        return nt(state, got_ref[g, :n, :n]) + push

    zero = jnp.zeros((shots, rank_max), F32)
    lax.fori_loop(0, fronts, step_forward, zero, unroll=True)
    lax.fori_loop(0, fronts, step_backward, zero, unroll=True)
    ahead = ahead_v[mine]
    behind = behind_v[mine]
    turned = nt(behind, last_ref[...])
    fetch.wait()
    rd_last = nn(next_ref[...], dinv_v[...], HIGH)
    scale = 1.0 / (shots * ranks_of_rhs)
    for k in range(blocks):
        columns = slice(k * width, (k + 1) * width)
        s = s_ref[k, :shots] + nn(ahead, s_ref[k, shots:])
        wave = wave_ref[:, columns] - nn(s, ld_ref[k], HIGH)
        if k + 1 < blocks:
            t = t_ref[k]
            arriving = t[:shots] + nn(ahead, t[shots : shots + n]) + nn(turned, t[shots + n :])
            rd = rd_ref[k]
        else:
            arriving = behind
            rd = rd_last
        adj = adj_ref[:, columns] - nn(s, e_ref[k], HIGH) - nn(arriving, rd, HIGH)
        wave_out[:, columns] = wave
        adj_out[:, columns] = adj
        image_v[:, columns] = jnp.sum(wave * adj, axis=0, keepdims=True) * scale

    groups = place_ref.shape[0]
    place = place_ref[...]
    high, low = place >> 7, place & (LANES - 1)
    out_rows = fronts * slot // LANES
    tops, rests, pick = [], [], []
    for j in range(groups):
        hit = one_hot_rows(out_rows, high[j : j + 1])
        top, rest = two_parts(jnp.where(hit, image_v[:, j * LANES : (j + 1) * LANES], 0.0))
        tops.append(top)
        rests.append(rest)
        pick.append(one_hot_rows(LANES, low[j : j + 1]).astype(F32).astype(BF16))
    table = jnp.concatenate([jnp.concatenate(tops, axis=1), jnp.concatenate(rests, axis=1)], axis=0)
    packed = nt(table, jnp.concatenate(pick, axis=1), None)
    packed = packed[:out_rows] + packed[out_rows:]
    each = slot // LANES
    for g in range(fronts):
        for r in range(ranks_of_rhs):
            image_out[g * ranks_of_rhs + r] = packed[g * each : (g + 1) * each]


def gather_kernel(fronts, slot, ranks_of_rhs, rank_max, got_ref, terms_ref, out_ref):
    each = slot // LANES
    out_rows = MC_DEV // LANES
    tops, rests, pick = [], [], []
    for g in range(fronts):
        terms = terms_ref[g * ranks_of_rhs]
        for r in range(1, ranks_of_rhs):
            terms = terms + terms_ref[g * ranks_of_rhs + r]
        cells = got_ref[g, rank_max : rank_max + each].astype(jnp.int32)
        high, low = cells >> 7, cells & (LANES - 1)
        for j in range(each):
            hit = one_hot_rows(out_rows, high[j : j + 1])
            top, rest = two_parts(jnp.where(hit, terms[j : j + 1], 0.0))
            tops.append(top)
            rests.append(rest)
            pick.append(one_hot_rows(LANES, low[j : j + 1]).astype(F32).astype(BF16))
    table = jnp.concatenate([jnp.concatenate(tops, axis=1), jnp.concatenate(rests, axis=1)], axis=0)
    found = nt(table, jnp.concatenate(pick, axis=1), None)
    out_ref[...] = found[:out_rows] + found[out_rows:]


def body(signs, sources, dinv, u_fac, v_fac, ranks, dobs, cellmap):
    shots = signs.shape[0]
    blocks, width, rank_max = u_fac.shape
    rows = blocks * width
    fronts = lax.axis_size("front")
    rhs = lax.axis_size("rhs")
    cap = 2 * rows // fronts
    slot = (cap + LANES - 1) // LANES * LANES
    each = slot // LANES
    packed_rows = fronts * each
    groups = rows // LANES
    tall = (rank_max + each + 7) // 8 * 8
    front = lax.axis_index("front").astype(jnp.int32).reshape(1)
    ut = jnp.swapaxes(u_fac, 1, 2)
    vt = jnp.swapaxes(v_fac, 1, 2)
    first = jnp.where(jnp.arange(rank_max)[:, None] < ranks[0], vt[0], 0.0)
    following = from_behind(first, "front", -1)

    smem = pl.BlockSpec(memory_space=pltpu.SMEM)
    vmem = pl.BlockSpec(memory_space=pltpu.VMEM)
    hbm = pl.BlockSpec(memory_space=pl.ANY)

    def shape(*dims):
        return jax.ShapeDtypeStruct(dims, F32)

    wave, adj, ld, e, rd, s, t, back, place, offset = pl.pallas_call(
        functools.partial(prep_kernel, fronts, slot),
        name="prep",
        out_shape=(
            shape(shots, rows),
            shape(shots, rows),
            shape(blocks, rank_max, width),
            shape(blocks, rank_max, width),
            shape(blocks - 1, rank_max, width),
            shape(blocks, shots + rank_max, rank_max),
            shape(blocks - 1, shots + 2 * rank_max, rank_max),
            shape(shots + rank_max, rank_max),
            jax.ShapeDtypeStruct((groups, LANES), jnp.int32),
            shape(packed_rows, LANES),
        ),
        in_specs=[smem, smem] + [hbm] * 7,
        out_specs=[vmem] * 10,
        scratch_shapes=[
            pltpu.VMEM(signs.shape, signs.dtype),
            pltpu.VMEM(sources.shape, sources.dtype),
            pltpu.VMEM(dinv.shape, dinv.dtype),
            pltpu.VMEM(ut.shape, ut.dtype),
            pltpu.VMEM(vt.shape, vt.dtype),
            pltpu.VMEM(dobs.shape, dobs.dtype),
            pltpu.VMEM((groups, LANES), cellmap.dtype),
            pltpu.SemaphoreType.DMA((5,)),
            pltpu.SemaphoreType.DMA((2, blocks)),
        ],
        cost_estimate=pl.CostEstimate(flops=400_000_000, bytes_accessed=6_000_000, transcendentals=0),
    )(front, ranks, signs, sources, dinv, ut, vt, dobs, cellmap.reshape(-1, LANES))

    send, last = pl.pallas_call(
        functools.partial(send_kernel, fronts, slot),
        name="send",
        out_shape=(shape(fronts, tall, LANES), shape(rank_max, rank_max)),
        in_specs=[vmem] * 6,
        out_specs=[vmem] * 2,
    )(wave, ld, s, following, back, offset)

    got = lax.all_to_all(send, "front", 0, 0)

    wave, adj, image = pl.pallas_call(
        functools.partial(solve_kernel, fronts, slot, rhs),
        name="solve",
        out_shape=(shape(shots, rows), shape(shots, rows), shape(fronts * rhs, each, LANES)),
        in_specs=[smem] + [vmem] * 11 + [hbm],
        out_specs=[vmem] * 3,
        scratch_shapes=[
            pltpu.VMEM((fronts, shots, rank_max), F32),
            pltpu.VMEM((fronts, shots, rank_max), F32),
            pltpu.VMEM((width, width), F32),
            pltpu.VMEM((1, rows), F32),
            pltpu.SemaphoreType.DMA,
        ],
    )(front, got, wave, adj, ld, e, rd, s, t, following, last, place, dinv)

    terms = lax.all_to_all(image, ("front", "rhs"), 0, 0)

    gradient = pl.pallas_call(
        functools.partial(gather_kernel, fronts, slot, rhs, rank_max),
        name="gather",
        out_shape=shape(MC_DEV // LANES, LANES),
        in_specs=[vmem] * 2,
        out_specs=vmem,
    )(got, terms)
    return (wave, adj, gradient.reshape(MC_DEV))


def solution(mesh):
    in_specs = (
        P("rhs", None),
        P(None, "front"),
        P("front", None, None),
        P("front", None, None),
        P("front", None, None),
        P("front"),
        P("rhs", "front"),
        P(),
    )
    out_specs = (P("rhs", "front"), P("rhs", "front"), P("front"))
    return jax.shard_map(body, mesh=mesh, in_specs=in_specs, out_specs=out_specs, check_vma=False)
```

time: 283 us -> 57.7 us (0.20)
  waiting for transfers between devices: 117 us -> 0.01 us
  matrix products: 67.7 us -> 0 us
  starting transfers between devices: 46.2 us -> 1.28 us
  Pallas kernels: 0 us -> 26.5 us
  blocking collectives: 5.77 us -> 26.7 us
  other arithmetic: 18 us -> 1.49 us
  between operations: 14.8 us -> 0.68 us
  local copies, waits for them, and re-layouts: 10.3 us -> 0.59 us
    unnamed x2 -> x0, waiting for transfers between devices: 70.3 us -> none
    dot_general x65 -> x0, matrix products: 67.7 us -> none  [the longest x8 15.6 us: forward_step(): jnp.dot(source - jnp.dot(state, left.T, precision=HIGHEST), inverse.T, pr...]
    ppermute x15 -> x1, waiting for transfers between devices: 47.1 us -> 0.01 us  [from_behind(): return lax.ppermute(array, axis, pairs)]
    ppermute x15 -> x1, starting transfers between devices: 46.1 us -> 1.28 us  [from_behind(): return lax.ppermute(array, axis, pairs)]
    all_to_all x0 -> x2, blocking collectives: none -> 26.7 us  [the longest x1 16.1 us: body(): got = lax.all_to_all(send, 'front', 0, 0)]
    pallas_call x0 -> x4, Pallas kernels: none -> 26.5 us  [the longest x1 15.8 us: body(): pl.pallas_call(functools.partial(prep_kernel, fronts, slot), name='prep',...]
    scatter-add x1 -> x0, other arithmetic: 11.9 us -> none  [body(): dense = jnp.zeros((model_cells,), jnp.float32).at[own_map].add(summed)]
    psum x1 -> x0, blocking collectives: 5.77 us -> none  [body(): summed = lax.psum(image, 'rhs')]
  transfers between devices with their start and end apart: 16 -> 1, of which waited for: 15 -> 0; matrix products, arithmetic and copies ran while one was open for 3% -> 0% of each run, Pallas kernels for 0% -> 28%
where the time goes in v1:
time: 57.7 us; the launch traced here: 57.3 us
  blocking collectives  26.7 us (46%)
  Pallas kernels  26.5 us (46%)
  other arithmetic  1.49 us (3%)
  starting transfers between devices  1.28 us (2%)
  between operations  0.68 us (1%)
  local copies, waits for them, and re-layouts  0.59 us (1%)
    all_to_all x1, blocking collectives, body(): got = lax.all_to_all(send, 'front', 0, 0)  16.1 us
    pallas_call x1, Pallas kernels, body(): pl.pallas_call(functools.partial(prep_kernel, fronts, slot), name='prep',...  15.8 us
    all_to_all x1, blocking collectives, body(): terms = lax.all_to_all(image, ('front', 'rhs'), 0, 0)  10.7 us
    pallas_call x1, Pallas kernels, body(): pl.pallas_call(functools.partial(solve_kernel, fronts, slot, rhs), name='...  6.24 us
    pallas_call x1, Pallas kernels, body(): pl.pallas_call(functools.partial(send_kernel, fronts, slot), name='send',...  2.25 us
    pallas_call x1, Pallas kernels, body(): pl.pallas_call(functools.partial(gather_kernel, fronts, slot, rhs, rank_m...  2.17 us
    ppermute x1, starting transfers between devices, from_behind(): return lax.ppermute(array, axis, pairs)  1.28 us
  transfers between devices with their start and end apart: 1, of which 0 were waited for; matrix products, arithmetic and copies ran while one was open for 0% of the time, Pallas kernels for 28%

profile of v1, /device:TPU:0, one launch (start us, length us, event | category | flops | bytes accessed | tf_op | source)
XLA Modules:
  0.0 57.3 jit_solution(660759843147115772)
XLA Ops:
  0.6 0.7 %iota_compare_fusion = pred[32]{0:T(512)(128)(4,1)S(1)} fusion(s32[]{:T(128)} %bitcast.16), kind=kLoop, calls=%fused_computation.2 | loop fusion | flops 32 | bytes 36 | tf_op jit(solution)/shard_map/lt | solution.py:285
  1.3 0.8 %fusion = f32[32,256]{1,0:T(8,128)S(1)} fusion(f32[8,32,256]{2,1,0:T(8,128)} %bitcast.11, pred[32]{0:T(512)(128)(4,1)S(1)} %iota_compare_fusion), kind=kLoop, calls=%fused_computation.1 | loop fusion | flops 8192 | bytes 65568 | tf_op jit(solution)/shard_map/jit(_where)/select_n | solution.py:285
  2.1 1.3 %collective-permute-start = (f32[32,256]{1,0:T(8,128)S(1)}, f32[32,256]{1,0:T(8,128)S(1)}, u32[]{:S(2)}, u32[]{:S(2)}) collective-permute-start(f32[32,256]{1,0:T(8,128)S(1)} %fusion), channel_id=1, source_target_pairs={{4,0},{8,4},{12,8},{16,12},{20,16},{24,20},{28,24},{5,1},{9,5},{13... | collective-permute-start | bytes 98312 | tf_op jit(solution)/shard_map/ppermute | solution.py:42
  3.4 15.8 %prep.1 = (f32[32,2048]{1,0:T(8,128)}, f32[32,2048]{1,0:T(8,128)}, f32[8,32,256]{2,1,0:T(8,128)}, f32[8,32,256]{2,1,0:T(8,128)}, f32[7,32,256]{2,1,0:T(8,128)}, ...) custom-call(s32[1]{0:T(128)} %bitcast.front_ref, ...), custom_call_target="tpu_custom_call" | custom-call | flops 400000000 | bytes 6000000 | tf_op jit(solution)/shard_map/prep/pallas_call | solution.py:295
  19.3 0.0 collective-permute-done.next_ref
  19.3 0.0 copy-start
  19.3 0.6 %copy-done = f32[32,256]{1,0:T(8,128)} copy-done((f32[32,256]{1,0:T(8,128)}, f32[32,256]{1,0:T(8,128)S(1)}, u32[]{:S(2)}) %copy-start) | copy-done | bytes 32792
  19.9 2.3 %send.1 = (f32[8,40,128]{2,1,0:T(8,128)}, f32[32,32]{1,0:T(8,128)}) custom-call(f32[32,2048]{1,0:T(8,128)} %get-tuple-element.18.wave_ref, f32[8,32,256]{2,1,0:T(8,128)} %get-tuple-element.19.ld_ref, f32[8,64,32]{2,1,0:T(8,128)} %get-tuple-element.20.s_ref, f32[32,256]{1,0:T(8,128)} %copy-done, f32[64,32]{1,0:T(8,128)} %get-tuple-element.21.back_ref, ...), custom_call_target="tpu_custom_call" | custom-call | tf_op jit(solution)/shard_map/send/pallas_call | solution.py:326
  22.1 16.1 %all_to_all.10.got_ref = f32[8,40,128]{2,1,0:T(8,128)} all-to-all(f32[8,40,128]{2,1,0:T(8,128)} %get-tuple-element.23), channel_id=1, replica_groups=mesh['front'=8,'rhs'=4] {'front'}, dimensions={0} | all-to-all | bytes 327680 | tf_op jit(solution)/shard_map/all_to_all | solution.py:334
  38.2 6.2 %solve.1 = (f32[32,2048]{1,0:T(8,128)}, f32[32,2048]{1,0:T(8,128)}, f32[32,4,128]{2,1,0:T(4,128)}) custom-call(s32[1]{0:T(128)} %bitcast.front_ref, f32[8,40,128]{2,1,0:T(8,128)} %all_to_all.10.got_ref, f32[32,2048]{1,0:T(8,128)} %get-tuple-element.18.wave_ref, f32[32,2048]{1,0:T(8,128)} %get-tuple-element.24.adj_ref, ...), custom_call_target="tpu_custom_call" | custom-call | tf_op jit(solution)/shard_map/solve/pallas_call | solution.py:336
  44.4 10.7 %all_to_all.11.terms_ref = f32[32,4,128]{2,1,0:T(4,128)} all-to-all(f32[32,4,128]{2,1,0:T(4,128)} %get-tuple-element.32), channel_id=1, replica_groups=mesh['front'=8,'rhs'=4] {'front','rhs'}, dimensions={0} | all-to-all | bytes 131072 | tf_op jit(solution)/shard_map/all_to_all | solution.py:351
  55.1 2.2 %gather.1 = f32[64,128]{1,0:T(8,128)} custom-call(f32[8,40,128]{2,1,0:T(8,128)} %all_to_all.10.got_ref, f32[32,4,128]{2,1,0:T(4,128)} %all_to_all.11.terms_ref), custom_call_target="tpu_custom_call" | custom-call | tf_op jit(solution)/shard_map/gather/pallas_call | solution.py:353
Async XLA Ops:
  2.1 17.1 %collective-permute-start = (f32[32,256]{1,0:T(8,128)S(1)}, f32[32,256]{1,0:T(8,128)S(1)}, u32[]{:S(2)}, u32[]{:S(2)}) collective-permute-start(f32[32,256]{1,0:T(8,128)S(1)} %fusion), channel_id=1, source_target_pairs={{4,0},{8,4},{12,8},{16,12},{20,16},{24,20},{28,24},{5,1},{9,5},{13... | collective-permute-start | bytes 98312 | tf_op jit(solution)/shard_map/ppermute | solution.py:42
  19.3 0.6 %copy-start = (f32[32,256]{1,0:T(8,128)}, f32[32,256]{1,0:T(8,128)S(1)}, u32[]{:S(2)}) copy-start(f32[32,256]{1,0:T(8,128)S(1)} %collective-permute-done.next_ref) | copy-start | bytes 98308

commit v2 on v0

v2 whole, which is shorter than its diff:
```python
import functools

import jax
import jax.numpy as jnp
from jax import lax
from jax.experimental import pallas as pl
from jax.experimental.pallas import tpu as pltpu
from jax.sharding import PartitionSpec as P

MC_DEV = 8192
LANES = 128
F32 = jnp.float32
BF16 = jnp.bfloat16
NN = (((1,), (0,)), ((), ()))
NT = (((1,), (1,)), ((), ()))


def dot(a, b, dims=NN):
    return lax.dot_general(a, b, dims, preferred_element_type=F32)


def parts(x):
    top = x.astype(BF16)
    return top, (x - top.astype(F32)).astype(BF16)


def dot3(a, b, dims=NN):
    rows = a[0].shape[0]
    first = dot(jnp.concatenate(a, axis=0), b[0], dims)
    return first[:rows] + first[rows:] + dot(a[0], b[1], dims)


def rows_of(pair, start, stop):
    return pair[0][start:stop], pair[1][start:stop]


def hits(count, index):
    return lax.broadcasted_iota(jnp.int32, (count, LANES), 0) == index


def as_ones(mask):
    return mask.astype(F32).astype(BF16)


def from_behind(array, axis, by):
    length = lax.axis_size(axis)
    pairs = [(i, i + by) for i in range(length) if 0 <= i + by < length]
    return lax.ppermute(array, axis, pairs)


def prep_kernel(
    ranks_hbm, signs_hbm, sources_hbm, dinv_hbm, ut_hbm, vt_hbm, dobs_hbm,
    y_ref, maps_ref, back_ref,
    ranks_ref, signs_v, sources_v, dinv_v, ut_v, vt_v, dobs_v, small_sem, block_sem,
):
    blocks, rank_max, width = ut_v.shape
    shots = signs_v.shape[0]
    small = [
        pltpu.make_async_copy(signs_hbm, signs_v, small_sem.at[0]),
        pltpu.make_async_copy(ut_hbm, ut_v, small_sem.at[1]),
        pltpu.make_async_copy(vt_hbm, vt_v, small_sem.at[2]),
        pltpu.make_async_copy(dobs_hbm, dobs_v, small_sem.at[3]),
        pltpu.make_async_copy(ranks_hbm, ranks_ref, small_sem.at[4]),
    ]
    large = []
    for k in range(blocks):
        columns = pl.ds(k * width, width)
        large.append(
            [
                pltpu.make_async_copy(sources_hbm.at[:, columns], sources_v.at[:, columns], block_sem.at[0, k]),
                pltpu.make_async_copy(dinv_hbm.at[k], dinv_v.at[k], block_sem.at[1, k]),
            ]
        )
    for copy in small + [copy for pair in large for copy in pair]:
        copy.start()
    for copy in small:
        copy.wait()

    sign = signs_v[...].astype(F32).astype(BF16)
    rank_row = lax.broadcasted_iota(jnp.int32, (rank_max, width), 0)
    unit_row = lax.broadcasted_iota(jnp.int32, (rank_max, rank_max), 0)
    unit_lane = lax.broadcasted_iota(jnp.int32, (rank_max, rank_max), 1)
    unit = (unit_row == unit_lane).astype(F32)
    nothing = jnp.zeros((rank_max, rank_max), F32)
    state = jnp.concatenate([jnp.zeros((shots, rank_max), F32), unit], axis=0)
    back = None
    for k in range(blocks):
        columns = slice(k * width, (k + 1) * width)
        for copy in large[k]:
            copy.wait()
        source = dot(sign, sources_v[:, columns])
        inverse = parts(dinv_v[k])
        left = jnp.where(rank_row < ranks_ref[k], ut_v[k], 0.0)
        swept = dot3(parts(jnp.concatenate([source, left], axis=0)), inverse, NT)
        y_ref[k] = swept
        residual = swept[:shots] - dobs_v[:, columns].astype(F32)
        swept = parts(swept)
        ld = rows_of(swept, shots, None)
        residual = parts(residual)
        both = tuple(jnp.concatenate([r, l], axis=0) for r, l in zip(residual, ld))
        seen = dot3(both, ld, NT)
        maps_ref[k, :, :rank_max] = state
        pair = parts(state)
        push = jnp.concatenate([seen[:shots], nothing], axis=0) - dot3(pair, parts(seen[shots:]))
        maps_ref[k, :, rank_max : 2 * rank_max] = push
        if k == 0:
            back = push
        else:
            back = back + dot3(parts(push), rows_of(pair, shots, None), NT)
        if k + 1 < blocks:
            right = jnp.where(rank_row < ranks_ref[k + 1], vt_v[k + 1], 0.0)
            passed = dot3(swept, parts(right), NT)
            forward = -passed[shots:]
            maps_ref[k, :rank_max, 2 * rank_max : 3 * rank_max] = forward
            state = dot3(pair, parts(forward)) + jnp.concatenate([passed[:shots], nothing], axis=0)
    back_ref[...] = back


def send_kernel(fronts, y_ref, maps_ref, next_ref, back_ref, send_ref, last_ref):
    blocks = y_ref.shape[0]
    shots = y_ref.shape[1] - next_ref.shape[0]
    passed = dot3(parts(y_ref[blocks - 1]), parts(next_ref[...]), NT)
    forward = -passed[shots:]
    last_ref[...] = forward
    state = dot3(parts(maps_ref[blocks - 1, :, : forward.shape[0]]), parts(forward))
    back = back_ref[...]
    payload = jnp.concatenate(
        [state[shots:], state[:shots] + passed[:shots], back[shots:], back[:shots]], axis=1
    )
    for g in range(fronts):
        send_ref[g] = payload


def fields_kernel(
    fronts, slot, front_ref, y_ref, maps_ref, next_ref, last_ref, map_hbm, dinv_hbm, vt_hbm, dobs_hbm, ranks_hbm,
    wave_ref, wave_top, wave_rest, adj_ref, ahead_top, ahead_rest, behind_top, behind_rest, hit_ref, pick_ref,
    map_v, dinv_v, vt_v, dobs_v, ranks_ref, sem, block_sem,
):
    blocks, n, width = vt_v.shape
    shots = dobs_v.shape[0]
    groups = map_v.shape[0]
    start = pl.multiple_of(front_ref[0] * groups, groups)
    fetch = [
        pltpu.make_async_copy(vt_hbm, vt_v, sem.at[0]),
        pltpu.make_async_copy(dobs_hbm, dobs_v, sem.at[1]),
        pltpu.make_async_copy(ranks_hbm, ranks_ref, sem.at[2]),
        pltpu.make_async_copy(map_hbm.at[pl.ds(start, groups)], map_v, sem.at[3]),
    ]
    for copy in fetch:
        copy.start()
    large = [pltpu.make_async_copy(dinv_hbm.at[k], dinv_v.at[k], block_sem.at[k]) for k in range(blocks)]
    for copy in large:
        copy.start()

    unit_row = lax.broadcasted_iota(jnp.int32, (n, n), 0)
    unit_lane = lax.broadcasted_iota(jnp.int32, (n, n), 1)
    unit = (unit_row == unit_lane).astype(F32)
    nothing = jnp.zeros((n, n), F32)
    state = jnp.concatenate([jnp.zeros((shots + n, n), F32), unit], axis=0)
    backs = [None] * blocks
    for k in range(blocks - 1, 0, -1):
        backs[k] = state
        factor = parts(last_ref[...] if k + 1 == blocks else maps_ref[k, :n, 2 * n : 3 * n])
        state = dot3(parts(state), factor, NT) + jnp.concatenate([maps_ref[k, :, n : 2 * n], nothing], axis=0)
    backs[0] = state
    for copy in fetch:
        copy.wait()
    rank_row = lax.broadcasted_iota(jnp.int32, (n, width), 0)

    for k in range(blocks):
        columns = slice(k * width, (k + 1) * width)
        if k + 1 < blocks:
            right = jnp.where(rank_row < ranks_ref[k + 1], vt_v[k + 1], 0.0)
        else:
            right = next_ref[...]
        residual = y_ref[k, :shots] - dobs_v[:, columns].astype(F32)
        rows = jnp.concatenate([residual, y_ref[k, shots:], right], axis=0)
        large[k].wait()
        returned = dot3(parts(rows), parts(dinv_v[k]))
        ahead = parts(maps_ref[k, :, :n])
        wave = dot3(ahead, parts(y_ref[k, shots:]))
        wave_ref[:, columns] = y_ref[k, :shots] - wave[:shots]
        wave_top[:, columns], wave_rest[:, columns] = parts(-wave[shots:])
        adj = dot3(ahead, parts(returned[shots : shots + n]))
        factor = parts(backs[k] if k else backs[0])
        late = dot3(factor, parts(returned[shots + n :]))
        adj_ref[:, columns] = returned[:shots] - adj[:shots] - late[:shots]
        ahead_top[:, columns], ahead_rest[:, columns] = parts(-adj[shots:] - late[shots : shots + n])
        behind_top[:, columns], behind_rest[:, columns] = parts(-late[shots + n :])

    owner = map_v[...] >> (MC_DEV.bit_length() - 1)
    member = jnp.concatenate([hits(fronts, owner[j : j + 1]).astype(F32) for j in range(groups)], axis=0)
    ranked = member * rank_in_order(member, fronts, groups, False)
    place = jnp.concatenate(
        [jnp.sum(ranked[j * fronts : (j + 1) * fronts], axis=0, keepdims=True) for j in range(groups)], axis=0
    ).astype(jnp.int32) + owner * slot
    out_rows = hit_ref.shape[0]
    for j in range(groups):
        lanes = slice(j * LANES, (j + 1) * LANES)
        at = place[j : j + 1]
        hit_ref[:, lanes] = as_ones(hits(out_rows, at >> 7))
        pick_ref[:, lanes] = as_ones(hits(LANES, at & (LANES - 1)))


def rank_in_order(member, stride, groups, blocked):
    count = member.shape[0]
    row = lax.broadcasted_iota(jnp.int32, (LANES, LANES), 0)
    lane = lax.broadcasted_iota(jnp.int32, (LANES, LANES), 1)
    member = member.astype(BF16)
    inside = dot(member, as_ones(row < lane))
    total = dot(member, jnp.ones((LANES, LANES), BF16))
    p = lax.broadcasted_iota(jnp.int32, (count, count), 0)
    q = lax.broadcasted_iota(jnp.int32, (count, count), 1)
    if blocked:
        shift = groups.bit_length() - 1
        same = (p >> shift) == (q >> shift)
    else:
        same = (p & (stride - 1)) == (q & (stride - 1))
    return inside + dot(as_ones(same & (q < p)), total.astype(BF16))


def solve_kernel(
    fronts, rhs, front_ref, got_ref, wave_ref, wave_top, wave_rest, adj_ref, ahead_top, ahead_rest,
    behind_top, behind_rest, hit_ref, pick_ref,
    wave_out, adj_out, image_out, token_ref,
    ahead_v, behind_v,
):
    shots, rows = wave_ref.shape
    n = wave_top.shape[0]
    mine = front_ref[0]
    token_ref[...] = jnp.zeros_like(token_ref)
    zero = jnp.zeros((shots, n), F32)

    state = zero
    ahead_v[0] = state
    pushes = [None]
    maps = [None]
    for g in range(fronts):
        if g > 0:
            ahead_v[g] = state
            pushes.append(dot3(parts(state), parts(got_ref[g, :, 2 * n : 3 * n])) + got_ref[g, :, 3 * n :])
            maps.append(parts(got_ref[g, :, :n]))
        if g + 1 < fronts:
            here = got_ref[g, :, n : 2 * n]
            state = here if g == 0 else dot3(parts(state), maps[g]) + here
    state = zero
    for g in range(fronts - 1, -1, -1):
        behind_v[g] = state
        if g > 0:
            here = pushes[g]
            state = here if g + 1 == fronts else dot3(parts(state), maps[g], NT) + here

    ahead = parts(ahead_v[mine])
    wave = wave_ref[...] + dot3(ahead, (wave_top[...], wave_rest[...]))
    wave_out[...] = wave
    adj = adj_ref[...] + dot3(ahead, (ahead_top[...], ahead_rest[...]))
    adj = adj + dot3(parts(behind_v[mine]), (behind_top[...], behind_rest[...]))
    adj_out[...] = adj
    image = jnp.sum(wave * adj, axis=0, keepdims=True) * (1.0 / (shots * rhs))
    top, rest = parts(image)
    hit = hit_ref[...]
    out_rows = hit.shape[0]
    table = jnp.concatenate([hit * top, hit * rest], axis=0)
    packed = dot(table, pick_ref[...], NT)
    packed = packed[:out_rows] + packed[out_rows:]
    each = out_rows // fronts
    for g in range(fronts):
        for r in range(rhs):
            image_out[g * rhs + r] = packed[g * each : (g + 1) * each]


def table_kernel(fronts, slot, front_ref, map_ref, token_ref, hit_ref, pick_ref):
    del token_ref
    each = slot // LANES
    count = map_ref.shape[0]
    groups = count // fronts
    cells = map_ref[...]
    mine = (cells >> (MC_DEV.bit_length() - 1)) == front_ref[0]
    rank = rank_in_order(mine.astype(F32), fronts, groups, True).astype(jnp.int32)
    rank = jnp.where(mine, rank, -1)
    local = cells & (MC_DEV - 1)
    coarse = (local >> 7).astype(F32)
    fine = (local & (LANES - 1)).astype(F32)
    high = rank >> 7
    low = jnp.where(mine, rank & (LANES - 1), -1)
    for f in range(fronts):
        table, pick = [], []
        for j in range(f * groups, (f + 1) * groups):
            hit = hits(each, high[j : j + 1])
            table.append(
                jnp.concatenate(
                    [jnp.where(hit, coarse[j : j + 1], 0.0), jnp.where(hit, fine[j : j + 1], 0.0)], axis=0
                ).astype(BF16)
            )
            pick.append(as_ones(hits(LANES, low[j : j + 1])))
        found = dot(jnp.concatenate(table, axis=1), jnp.concatenate(pick, axis=1), NT).astype(jnp.int32)
        for j in range(each):
            lanes = slice((f * each + j) * LANES, (f * each + j + 1) * LANES)
            hit_ref[:, lanes] = as_ones(hits(MC_DEV // LANES, found[j : j + 1]))
            pick_ref[:, lanes] = as_ones(hits(LANES, found[each + j : each + j + 1]))


def gather_kernel(fronts, rhs, terms_ref, hit_ref, pick_ref, out_ref):
    each = terms_ref.shape[1]
    rows = []
    for g in range(fronts):
        terms = terms_ref[g * rhs]
        for r in range(1, rhs):
            terms = terms + terms_ref[g * rhs + r]
        rows += [terms[j : j + 1] for j in range(each)]
    top, rest = parts(jnp.concatenate(rows, axis=1))
    hit = hit_ref[...]
    out_rows = hit.shape[0]
    found = dot(jnp.concatenate([hit * top, hit * rest], axis=0), pick_ref[...], NT)
    out_ref[...] = found[:out_rows] + found[out_rows:]


def body(signs, sources, dinv, u_fac, v_fac, ranks, dobs, cellmap):
    shots = signs.shape[0]
    blocks, width, n = u_fac.shape
    rows = blocks * width
    fronts = lax.axis_size("front")
    rhs = lax.axis_size("rhs")
    cap = 2 * rows // fronts
    slot = (cap + LANES - 1) // LANES * LANES
    each = slot // LANES
    groups = rows // LANES
    front = lax.axis_index("front").astype(jnp.int32).reshape(1)
    ut = jnp.swapaxes(u_fac, 1, 2)
    vt = jnp.swapaxes(v_fac, 1, 2)
    cells = cellmap.reshape(-1, LANES)
    live = jnp.clip(ranks[0] - jnp.arange(n, dtype=jnp.int32), 0, 1).astype(F32)
    following = from_behind(vt[0] * live[:, None], "front", -1)

    smem = pl.BlockSpec(memory_space=pltpu.SMEM)
    vmem = pl.BlockSpec(memory_space=pltpu.VMEM)
    hbm = pl.BlockSpec(memory_space=pltpu.HBM)

    def held(*arrays):
        return [pltpu.with_memory_space_constraint(a, pltpu.VMEM) for a in arrays]

    def far(*arrays):
        return [pltpu.with_memory_space_constraint(a, pltpu.HBM) for a in arrays]

    def cost(us):
        return pl.CostEstimate(flops=int(us * 1e9), bytes_accessed=int(us * 3e6), transcendentals=0)

    room = pltpu.CompilerParams(vmem_limit_bytes=24 * 2**20)

    y, maps, back = pl.pallas_call(
        prep_kernel,
        name="prep",
        out_shape=(
            pltpu.VMEM((blocks, shots + n, width), F32),
            pltpu.VMEM((blocks, shots + n, 4 * n), F32),
            pltpu.VMEM((shots + n, n), F32),
        ),
        in_specs=[hbm] * 7,
        out_specs=[vmem] * 3,
        scratch_shapes=[
            pltpu.SMEM(ranks.shape, ranks.dtype),
            pltpu.VMEM(signs.shape, signs.dtype),
            pltpu.VMEM(sources.shape, sources.dtype),
            pltpu.VMEM(dinv.shape, dinv.dtype),
            pltpu.VMEM(ut.shape, ut.dtype),
            pltpu.VMEM(vt.shape, vt.dtype),
            pltpu.VMEM(dobs.shape, dobs.dtype),
            pltpu.SemaphoreType.DMA((5,)),
            pltpu.SemaphoreType.DMA((2, blocks)),
        ],
        cost_estimate=cost(6),
        compiler_params=room,
    )(*far(ranks, signs, sources, dinv, ut, vt, dobs))

    send, last = pl.pallas_call(
        functools.partial(send_kernel, fronts),
        name="send",
        out_shape=(pltpu.VMEM((fronts, n, 4 * n), F32), pltpu.VMEM((n, n), F32)),
        in_specs=[vmem] * 4,
        out_specs=[vmem] * 2,
        cost_estimate=cost(0.5),
        compiler_params=room,
    )(*held(y, maps, following, back))

    got = lax.all_to_all(send, "front", 0, 0)

    fields = pl.pallas_call(
        functools.partial(fields_kernel, fronts, slot),
        name="fields",
        out_shape=(
            pltpu.VMEM((shots, rows), F32),
            pltpu.VMEM((n, rows), BF16),
            pltpu.VMEM((n, rows), BF16),
            pltpu.VMEM((shots, rows), F32),
            pltpu.VMEM((n, rows), BF16),
            pltpu.VMEM((n, rows), BF16),
            pltpu.VMEM((n, rows), BF16),
            pltpu.VMEM((n, rows), BF16),
            pltpu.VMEM((fronts * each, rows), BF16),
            pltpu.VMEM((LANES, rows), BF16),
        ),
        in_specs=[smem] + [vmem] * 4 + [hbm] * 5,
        out_specs=[vmem] * 10,
        scratch_shapes=[
            pltpu.VMEM((groups, LANES), cells.dtype),
            pltpu.VMEM(dinv.shape, dinv.dtype),
            pltpu.VMEM(vt.shape, vt.dtype),
            pltpu.VMEM(dobs.shape, dobs.dtype),
            pltpu.SMEM(ranks.shape, ranks.dtype),
            pltpu.SemaphoreType.DMA((4,)),
            pltpu.SemaphoreType.DMA((blocks,)),
        ],
        cost_estimate=cost(5),
        compiler_params=room,
    )(front, *held(y, maps, following, last), *far(cells, dinv, vt, dobs, ranks))

    wave, adj, image, token = pl.pallas_call(
        functools.partial(solve_kernel, fronts, rhs),
        name="solve",
        out_shape=(
            pltpu.VMEM((shots, rows), F32),
            pltpu.VMEM((shots, rows), F32),
            pltpu.VMEM((fronts * rhs, each, LANES), F32),
            pltpu.VMEM((8, LANES), F32),
        ),
        in_specs=[smem] + [vmem] * 11,
        out_specs=[vmem] * 4,
        scratch_shapes=[
            pltpu.VMEM((fronts, shots, n), F32),
            pltpu.VMEM((fronts, shots, n), F32),
        ],
        cost_estimate=cost(3),
        compiler_params=room,
    )(front, *held(got, *fields))

    terms = lax.all_to_all(image, ("front", "rhs"), 0, 0)

    hit, pick = pl.pallas_call(
        functools.partial(table_kernel, fronts, slot),
        name="tables",
        out_shape=(
            pltpu.VMEM((MC_DEV // LANES, fronts * slot), BF16),
            pltpu.VMEM((LANES, fronts * slot), BF16),
        ),
        in_specs=[smem, vmem, vmem],
        out_specs=[vmem] * 2,
        cost_estimate=cost(4),
        compiler_params=room,
    )(front, *far(cells), *held(token))

    gradient = pl.pallas_call(
        functools.partial(gather_kernel, fronts, rhs),
        name="gather",
        out_shape=jax.ShapeDtypeStruct((MC_DEV // LANES, LANES), F32),
        in_specs=[vmem] * 3,
        out_specs=vmem,
        cost_estimate=cost(1),
        compiler_params=room,
    )(*held(terms, hit, pick))
    return (wave, adj, gradient.reshape(MC_DEV))


def solution(mesh):
    in_specs = (
        P("rhs", None),
        P(None, "front"),
        P("front", None, None),
        P("front", None, None),
        P("front", None, None),
        P("front"),
        P("rhs", "front"),
        P(),
    )
    out_specs = (P("rhs", "front"), P("rhs", "front"), P("front"))
    return jax.shard_map(body, mesh=mesh, in_specs=in_specs, out_specs=out_specs, check_vma=False)
```

time: 283 us -> 46.5 us (0.16)
  waiting for transfers between devices: 117 us -> 4.29 us
  matrix products: 67.7 us -> 0 us
  starting transfers between devices: 46.2 us -> 14.7 us
  Pallas kernels: 0 us -> 23.6 us
  other arithmetic: 18 us -> 1.49 us
  between operations: 14.8 us -> 0.69 us
  local copies, waits for them, and re-layouts: 10.3 us -> 1.41 us
  blocking collectives: 5.77 us -> 0 us
    unnamed x2 -> x0, waiting for transfers between devices: 70.3 us -> none
    dot_general x65 -> x0, matrix products: 67.7 us -> none  [the longest x8 15.6 us: forward_step(): jnp.dot(source - jnp.dot(state, left.T, precision=HIGHEST), inverse.T, pr...]
    ppermute x15 -> x1, waiting for transfers between devices: 47.1 us -> 0.01 us  [from_behind(): return lax.ppermute(array, axis, pairs)]
    ppermute x15 -> x1, starting transfers between devices: 46.1 us -> 1.28 us  [from_behind(): return lax.ppermute(array, axis, pairs)]
    pallas_call x0 -> x6, Pallas kernels: none -> 23.6 us  [the longest x1 9.45 us: body(): pl.pallas_call(prep_kernel, name='prep', out_shape=(pltpu.VMEM((blocks, s...]
    all_to_all x0 -> x2, starting transfers between devices: none -> 13.4 us  [the longest x1 8.43 us: body(): got = lax.all_to_all(send, 'front', 0, 0)]
    scatter-add x1 -> x0, other arithmetic: 11.9 us -> none  [body(): dense = jnp.zeros((model_cells,), jnp.float32).at[own_map].add(summed)]
    psum x1 -> x0, blocking collectives: 5.77 us -> none  [body(): summed = lax.psum(image, 'rhs')]
  transfers between devices with their start and end apart: 16 -> 3, of which waited for: 15 -> 2; matrix products, arithmetic and copies ran while one was open for 3% -> 3% of each run, Pallas kernels for 0% -> 40%
where the time goes in v2:
time: 46.5 us; the launch traced here: 46.1 us
  Pallas kernels  23.6 us (51%)
  starting transfers between devices  14.7 us (32%)
  waiting for transfers between devices  4.29 us (9%)
  other arithmetic  1.49 us (3%)
  local copies, waits for them, and re-layouts  1.41 us (3%)
  between operations  0.69 us (1%)
    pallas_call x1, Pallas kernels, body(): pl.pallas_call(prep_kernel, name='prep', out_shape=(pltpu.VMEM((blocks, s...  9.45 us
    all_to_all x1, starting transfers between devices, body(): got = lax.all_to_all(send, 'front', 0, 0)  8.43 us
    pallas_call x1, Pallas kernels, body(): pl.pallas_call(functools.partial(fields_kernel, fronts, slot), name='fiel...  6.21 us
    all_to_all x1, starting transfers between devices, body(): terms = lax.all_to_all(image, ('front', 'rhs'), 0, 0)  4.97 us
    all_to_all x1, waiting for transfers between devices, body(): terms = lax.all_to_all(image, ('front', 'rhs'), 0, 0)  3.15 us
    pallas_call x1, Pallas kernels, body(): pl.pallas_call(functools.partial(solve_kernel, fronts, rhs), name='solve'...  2.97 us
    pallas_call x1, Pallas kernels, body(): pl.pallas_call(functools.partial(table_kernel, fronts, slot), name='table...  2.84 us
    unnamed x2, local copies, waits for them, and re-layouts  1.41 us
  transfers between devices with their start and end apart: 3, of which 2 were waited for; matrix products, arithmetic and copies ran while one was open for 3% of the time, Pallas kernels for 40%

profile of v2, /device:TPU:0, one launch (start us, length us, event | category | flops | bytes accessed | tf_op | source)
XLA Modules:
  0.0 46.1 jit_solution(16570362817662367354)
XLA Ops:
  0.6 0.7 %clamp_convert_fusion = f32[32]{0:T(128)S(1)} fusion(s32[]{:T(128)} %bitcast.17), kind=kLoop, calls=%fused_computation.2 | loop fusion | flops 96 | bytes 132 | tf_op jit(solution)/shard_map/convert_element_type | solution.py:332
  1.3 0.8 %fusion = f32[32,256]{1,0:T(8,128)S(1)} fusion(f32[8,32,256]{2,1,0:T(8,128)} %bitcast.11, f32[32]{0:T(128)S(1)} %clamp_convert_fusion), kind=kLoop, calls=%fused_computation.1 | loop fusion | flops 8192 | bytes 65664 | tf_op jit(solution)/shard_map/mul | solution.py:333
  2.1 1.3 %collective-permute-start = (f32[32,256]{1,0:T(8,128)S(1)}, f32[32,256]{1,0:T(8,128)S(1)}, u32[]{:S(2)}, u32[]{:S(2)}) collective-permute-start(f32[32,256]{1,0:T(8,128)S(1)} %fusion), channel_id=1, source_target_pairs={{4,0},{8,4},{12,8},{16,12},{20,16},{24,20},{28,24},{5,1},{9,5},{13... | collective-permute-start | bytes 98312 | tf_op jit(solution)/shard_map/ppermute | solution.py:48
  3.4 9.4 %prep.1 = (f32[8,64,256]{2,1,0:T(8,128)S(1)}, f32[8,64,128]{2,1,0:T(8,128)S(1)}, f32[64,32]{1,0:T(8,128)S(1)}) custom-call(s32[8]{0:T(128)} %ranks_hbm.3, s32[32,512]{1,0:T(8,128)} %signs_hbm.1, bf16[512,2048]{1,0:T(8,128)(2,1)} %sources_hbm.1, f32[8,256,256]{2,1,0:T(8,128)} %dinv_hbm.3, f32[8,32,256]{2,1,0:T(8,128)} %bitcast.14, f32[8,32,256]{2,1,0:T(8,128)} %bitcast.12, ...), custom_call_target="tpu_custom_call" | custom-call | flops 6000000000 | bytes 18000000 | tf_op jit(solution)/shard_map/prep/pallas_call | solution.py:350
  12.9 0.0 collective-permute-done.next_ref
  12.9 1.0 %send.1 = (f32[8,32,128]{2,1,0:T(8,128)}, f32[32,32]{1,0:T(8,128)S(1)}) custom-call(f32[8,64,256]{2,1,0:T(8,128)S(1)} %get-tuple-element.24.y_ref, f32[8,64,128]{2,1,0:T(8,128)S(1)} %get-tuple-element.25.maps_ref, f32[32,256]{1,0:T(8,128)S(1)} %collective-permute-done.next_ref, f32[64,32]{1,0:T(8,128)S(1)} %get-tuple-element.26.back_ref), custom_call_target="tpu_custom_call" | custom-call | flops 500000000 | bytes 1500000 | tf_op jit(solution)/shard_map/send/pallas_call | solution.py:375
  13.9 8.4 %all-to-all-start = ((f32[8,32,128]{2,1,0:T(8,128)}), f32[8,32,128]{2,1,0:T(8,128)S(1)}, u32[]{:S(2)}, u32[]{:S(2)}) async-start(f32[8,32,128]{2,1,0:T(8,128)} %get-tuple-element.27), calls=%async_computation | async-start | bytes 262144 | tf_op jit(solution)/shard_map/all_to_all | solution.py:385
  22.4 6.2 %fields.1 = (f32[32,2048]{1,0:T(8,128)S(1)}, bf16[32,2048]{1,0:T(8,128)(2,1)S(1)}, bf16[32,2048]{1,0:T(8,128)(2,1)S(1)}, f32[32,2048]{1,0:T(8,128)S(1)}, bf16[32...) custom-call(s32[1]{0:T(128)} %bitcast.front_ref, ...), custom_call_target="tpu_custom_call" | custom-call | flops 5000000000 | bytes 15000000 | tf_op jit(solution)/shard_map/fields/pallas_call | solution.py:387
  28.6 1.1 %all-to-all-done.got_ref = f32[8,32,128]{2,1,0:T(8,128)S(1)} async-done(((f32[8,32,128]{2,1,0:T(8,128)}), f32[8,32,128]{2,1,0:T(8,128)S(1)}, u32[]{:S(2)}, u32[]{:S(2)}) %all-to-all-start) | async-done | bytes 131104 | tf_op jit(solution)/shard_map/all_to_all | solution.py:385
  29.7 3.0 %solve.1 = (f32[32,2048]{1,0:T(8,128)S(1)}, f32[32,2048]{1,0:T(8,128)S(1)}, f32[32,4,128]{2,1,0:T(4,128)}, f32[8,128]{1,0:T(8,128)S(1)}) custom-call(s32[1]{0:T(128)} %bitcast.front_ref, f32[8,32,128]{2,1,0:T(8,128)S(1)} %all-to-all-done.got_ref, f32[32,2048]{1,0:T(8,128)S(1)} %get-tuple-element.29.wave_ref, ...), custom_call_target="tpu_custom_call" | custom-call | flops 3000000000 | bytes 9000000 | tf_op jit(solution)/shard_map/solve/pallas_call | solution.py:417
  32.7 5.0 %all-to-all-start.1 = ((f32[32,4,128]{2,1,0:T(4,128)}), f32[32,4,128]{2,1,0:T(4,128)S(1)}, u32[]{:S(2)}, u32[]{:S(2)}) async-start(f32[32,4,128]{2,1,0:T(4,128)} %get-tuple-element.41), calls=%async_computation.1 | async-start | bytes 131072 | tf_op jit(solution)/shard_map/all_to_all | solution.py:436
  37.6 2.8 %tables.1 = (bf16[64,4096]{1,0:T(8,128)(2,1)S(1)}, bf16[128,4096]{1,0:T(8,128)(2,1)S(1)}) custom-call(s32[1]{0:T(128)} %bitcast.front_ref, s32[128,128]{1,0:T(8,128)} %bitcast.16, f32[8,128]{1,0:T(8,128)S(1)} %get-tuple-element.42.token_ref), custom_call_target="tpu_custom_call" | custom-call | flops 4000000000 | bytes 12000000 | tf_op jit(solution)/shard_map/tables/pallas_call | solution.py:438
  40.5 0.7 %copy.11 = f32[32,2048]{1,0:T(8,128)} copy(f32[32,2048]{1,0:T(8,128)S(1)} %get-tuple-element.45) | data formatting | bytes 524288
  41.2 0.7 %copy.12 = f32[32,2048]{1,0:T(8,128)} copy(f32[32,2048]{1,0:T(8,128)S(1)} %get-tuple-element.46) | data formatting | bytes 524288
  41.9 3.2 %all-to-all-done.1.terms_ref = f32[32,4,128]{2,1,0:T(4,128)S(1)} async-done(((f32[32,4,128]{2,1,0:T(4,128)}), f32[32,4,128]{2,1,0:T(4,128)S(1)}, u32[]{:S(2)}, u32[]{:S(2)}) %all-to-all-start.1) | async-done | bytes 65568 | tf_op jit(solution)/shard_map/all_to_all | solution.py:436
  45.1 1.1 %gather.1 = f32[64,128]{1,0:T(8,128)} custom-call(f32[32,4,128]{2,1,0:T(4,128)S(1)} %all-to-all-done.1.terms_ref, bf16[64,4096]{1,0:T(8,128)(2,1)S(1)} %get-tuple-element.43.hit_ref, bf16[128,4096]{1,0:T(8,128)(2,1)S(1)} %get-tuple-element.44.pick_ref), custom_call_target="tpu_custom_call" | custom-call | flops 1000000000 | bytes 3000000 | tf_op jit(solution)/shard_map/gather/pallas_call | solution.py:451
Async XLA Ops:
  2.1 10.8 %collective-permute-start = (f32[32,256]{1,0:T(8,128)S(1)}, f32[32,256]{1,0:T(8,128)S(1)}, u32[]{:S(2)}, u32[]{:S(2)}) collective-permute-start(f32[32,256]{1,0:T(8,128)S(1)} %fusion), channel_id=1, source_target_pairs={{4,0},{8,4},{12,8},{16,12},{20,16},{24,20},{28,24},{5,1},{9,5},{13... | collective-permute-start | bytes 98312 | tf_op jit(solution)/shard_map/ppermute | solution.py:48
  13.9 15.8 %all-to-all-start = ((f32[8,32,128]{2,1,0:T(8,128)}), f32[8,32,128]{2,1,0:T(8,128)S(1)}, u32[]{:S(2)}, u32[]{:S(2)}) async-start(f32[8,32,128]{2,1,0:T(8,128)} %get-tuple-element.27), calls=%async_computation | async-start | bytes 262144 | tf_op jit(solution)/shard_map/all_to_all | solution.py:385
  32.7 12.4 %all-to-all-start.1 = ((f32[32,4,128]{2,1,0:T(4,128)}), f32[32,4,128]{2,1,0:T(4,128)S(1)}, u32[]{:S(2)}, u32[]{:S(2)}) async-start(f32[32,4,128]{2,1,0:T(4,128)} %get-tuple-element.41), calls=%async_computation.1 | async-start | bytes 131072 | tf_op jit(solution)/shard_map/all_to_all | solution.py:436

commit v3 on v2

--- a/solution.py
+++ b/solution.py
@@ -2,6 +2,7 @@
 
 import jax
 import jax.numpy as jnp
+import numpy as np
 from jax import lax
 from jax.experimental import pallas as pl
 from jax.experimental.pallas import tpu as pltpu
@@ -71,48 +72,73 @@
                 pltpu.make_async_copy(dinv_hbm.at[k], dinv_v.at[k], block_sem.at[1, k]),
             ]
         )
-    for copy in small + [copy for pair in large for copy in pair]:
+    early = small[:1] + [pair[0] for pair in large]
+    late = small[1:] + [pair[1] for pair in large]
+    for copy in early + late:
         copy.start()
-    for copy in small:
+    for copy in early:
         copy.wait()
 
     sign = signs_v[...].astype(F32).astype(BF16)
     rank_row = lax.broadcasted_iota(jnp.int32, (rank_max, width), 0)
-    unit_row = lax.broadcasted_iota(jnp.int32, (rank_max, rank_max), 0)
-    unit_lane = lax.broadcasted_iota(jnp.int32, (rank_max, rank_max), 1)
-    unit = (unit_row == unit_lane).astype(F32)
-    nothing = jnp.zeros((rank_max, rank_max), F32)
-    state = jnp.concatenate([jnp.zeros((shots, rank_max), F32), unit], axis=0)
+    products = {}
+    for k in range(blocks):
+        y_ref[k, :shots] = dot(sign, sources_v[:, k * width : (k + 1) * width])
+    for copy in late:
+        copy.wait()
+
+    def sweep(k):
+        left = jnp.where(rank_row < ranks_ref[k], ut_v[k], 0.0)
+        y_ref[k] = dot3(parts(jnp.concatenate([y_ref[k, :shots], left], axis=0)), parts(dinv_v[k]), NT)
+
+    def project(k):
+        swept = y_ref[k]
+        residual = parts(swept[:shots] - dobs_v[:, k * width : (k + 1) * width].astype(F32))
+        swept = parts(swept)
+        wave, ld = rows_of(swept, 0, shots), rows_of(swept, shots, None)
+        if k + 1 < blocks:
+            right = parts(jnp.where(rank_row < ranks_ref[k + 1], vt_v[k + 1], 0.0))
+        else:
+            right = parts(jnp.zeros((rank_max, width), F32))
+        rows = tuple(jnp.concatenate(three, axis=0) for three in zip(wave, residual, ld))
+        products[k] = dot3(rows, tuple(jnp.concatenate(two, axis=0) for two in zip(right, ld)), NT)
+
+    for k in range(blocks):
+        sweep(k)
+    for k in range(blocks):
+        project(k)
+
+    n = rank_max
+    nothing = jnp.zeros((n, n), F32)
+
+    def follow(span, k):
+        later = dot3(span, parts(steps[k][shots:]))
+        return jnp.concatenate([later[:shots] + steps[k][:shots], later[shots:]], axis=0)
+
+    steps = [jnp.concatenate([seen[:shots, :n], -seen[2 * shots :, :n]], axis=0) for seen in map(products.get, range(blocks))]
+    joint = {k: follow(parts(steps[k]), k + 1) for k in range(1, blocks - 2, 2)}
+    spans = [steps[0]]
+    for k in range(1, blocks - 1, 2):
+        pair = parts(spans[-1])
+        spans.append(follow(pair, k))
+        if k in joint:
+            later = dot3(pair, parts(joint[k][shots:]))
+            spans.append(jnp.concatenate([later[:shots] + joint[k][:shots], later[shots:]], axis=0))
     back = None
     for k in range(blocks):
-        columns = slice(k * width, (k + 1) * width)
-        for copy in large[k]:
-            copy.wait()
-        source = dot(sign, sources_v[:, columns])
-        inverse = parts(dinv_v[k])
-        left = jnp.where(rank_row < ranks_ref[k], ut_v[k], 0.0)
-        swept = dot3(parts(jnp.concatenate([source, left], axis=0)), inverse, NT)
-        y_ref[k] = swept
-        residual = swept[:shots] - dobs_v[:, columns].astype(F32)
-        swept = parts(swept)
-        ld = rows_of(swept, shots, None)
-        residual = parts(residual)
-        both = tuple(jnp.concatenate([r, l], axis=0) for r, l in zip(residual, ld))
-        seen = dot3(both, ld, NT)
-        maps_ref[k, :, :rank_max] = state
-        pair = parts(state)
-        push = jnp.concatenate([seen[:shots], nothing], axis=0) - dot3(pair, parts(seen[shots:]))
-        maps_ref[k, :, rank_max : 2 * rank_max] = push
+        seen = products[k]
+        push = jnp.concatenate([seen[shots : 2 * shots, n:], nothing], axis=0)
         if k == 0:
+            push = push - jnp.concatenate([nothing, seen[2 * shots :, n:]], axis=0)
             back = push
         else:
+            pair = parts(spans[k - 1])
+            push = push - dot3(pair, parts(seen[2 * shots :, n:]))
             back = back + dot3(parts(push), rows_of(pair, shots, None), NT)
         if k + 1 < blocks:
-            right = jnp.where(rank_row < ranks_ref[k + 1], vt_v[k + 1], 0.0)
-            passed = dot3(swept, parts(right), NT)
-            forward = -passed[shots:]
-            maps_ref[k, :rank_max, 2 * rank_max : 3 * rank_max] = forward
-            state = dot3(pair, parts(forward)) + jnp.concatenate([passed[:shots], nothing], axis=0)
+            maps_ref[k, :, :n] = spans[k]
+        maps_ref[k, :, n : 2 * n] = push
+        maps_ref[k, :n, 2 * n :] = seen[2 * shots :]
     back_ref[...] = back
 
 
@@ -122,7 +148,7 @@
     passed = dot3(parts(y_ref[blocks - 1]), parts(next_ref[...]), NT)
     forward = -passed[shots:]
     last_ref[...] = forward
-    state = dot3(parts(maps_ref[blocks - 1, :, : forward.shape[0]]), parts(forward))
+    state = dot3(parts(maps_ref[blocks - 2, :, : forward.shape[0]]), parts(forward))
     back = back_ref[...]
     payload = jnp.concatenate(
         [state[shots:], state[:shots] + passed[:shots], back[shots:], back[:shots]], axis=1
@@ -160,33 +186,11 @@
     backs = [None] * blocks
     for k in range(blocks - 1, 0, -1):
         backs[k] = state
-        factor = parts(last_ref[...] if k + 1 == blocks else maps_ref[k, :n, 2 * n : 3 * n])
+        factor = parts(last_ref[...] if k + 1 == blocks else -maps_ref[k, :n, 2 * n : 3 * n])
         state = dot3(parts(state), factor, NT) + jnp.concatenate([maps_ref[k, :, n : 2 * n], nothing], axis=0)
     backs[0] = state
     for copy in fetch:
         copy.wait()
-    rank_row = lax.broadcasted_iota(jnp.int32, (n, width), 0)
-
-    for k in range(blocks):
-        columns = slice(k * width, (k + 1) * width)
-        if k + 1 < blocks:
-            right = jnp.where(rank_row < ranks_ref[k + 1], vt_v[k + 1], 0.0)
-        else:
-            right = next_ref[...]
-        residual = y_ref[k, :shots] - dobs_v[:, columns].astype(F32)
-        rows = jnp.concatenate([residual, y_ref[k, shots:], right], axis=0)
-        large[k].wait()
-        returned = dot3(parts(rows), parts(dinv_v[k]))
-        ahead = parts(maps_ref[k, :, :n])
-        wave = dot3(ahead, parts(y_ref[k, shots:]))
-        wave_ref[:, columns] = y_ref[k, :shots] - wave[:shots]
-        wave_top[:, columns], wave_rest[:, columns] = parts(-wave[shots:])
-        adj = dot3(ahead, parts(returned[shots : shots + n]))
-        factor = parts(backs[k] if k else backs[0])
-        late = dot3(factor, parts(returned[shots + n :]))
-        adj_ref[:, columns] = returned[:shots] - adj[:shots] - late[:shots]
-        ahead_top[:, columns], ahead_rest[:, columns] = parts(-adj[shots:] - late[shots : shots + n])
-        behind_top[:, columns], behind_rest[:, columns] = parts(-late[shots + n :])
 
     owner = map_v[...] >> (MC_DEV.bit_length() - 1)
     member = jnp.concatenate([hits(fronts, owner[j : j + 1]).astype(F32) for j in range(groups)], axis=0)
@@ -200,6 +204,32 @@
         at = place[j : j + 1]
         hit_ref[:, lanes] = as_ones(hits(out_rows, at >> 7))
         pick_ref[:, lanes] = as_ones(hits(LANES, at & (LANES - 1)))
+
+    for copy in large:
+        copy.wait()
+    rank_row = lax.broadcasted_iota(jnp.int32, (n, width), 0)
+
+    for k in range(blocks):
+        columns = slice(k * width, (k + 1) * width)
+        if k + 1 < blocks:
+            right = jnp.where(rank_row < ranks_ref[k + 1], vt_v[k + 1], 0.0)
+        else:
+            right = next_ref[...]
+        residual = y_ref[k, :shots] - dobs_v[:, columns].astype(F32)
+        rows = jnp.concatenate([residual, y_ref[k, shots:], right], axis=0)
+        returned = dot3(parts(rows), parts(dinv_v[k]))
+        if k > 0:
+            ahead = maps_ref[k - 1, :, :n]
+        else:
+            ahead = jnp.concatenate([jnp.zeros((shots, n), F32), unit], axis=0)
+        wave = dot3(parts(ahead), parts(y_ref[k, shots:]))
+        wave_ref[:, columns] = y_ref[k, :shots] - wave[:shots]
+        wave_top[:, columns], wave_rest[:, columns] = parts(-wave[shots:])
+        enters = jnp.concatenate([jnp.concatenate([ahead, nothing], axis=0), backs[k]], axis=1)
+        adj = dot3(parts(enters), parts(returned[shots:]))
+        adj_ref[:, columns] = returned[:shots] - adj[:shots]
+        ahead_top[:, columns], ahead_rest[:, columns] = parts(-adj[shots : shots + n])
+        behind_top[:, columns], behind_rest[:, columns] = parts(-adj[shots + n :])
 
 
 def rank_in_order(member, stride, groups, blocked):
@@ -231,24 +261,34 @@
     token_ref[...] = jnp.zeros_like(token_ref)
     zero = jnp.zeros((shots, n), F32)
 
-    state = zero
-    ahead_v[0] = state
-    pushes = [None]
-    maps = [None]
-    for g in range(fronts):
-        if g > 0:
-            ahead_v[g] = state
-            pushes.append(dot3(parts(state), parts(got_ref[g, :, 2 * n : 3 * n])) + got_ref[g, :, 3 * n :])
-            maps.append(parts(got_ref[g, :, :n]))
-        if g + 1 < fronts:
-            here = got_ref[g, :, n : 2 * n]
-            state = here if g == 0 else dot3(parts(state), maps[g]) + here
-    state = zero
-    for g in range(fronts - 1, -1, -1):
-        behind_v[g] = state
-        if g > 0:
-            here = pushes[g]
-            state = here if g + 1 == fronts else dot3(parts(state), maps[g], NT) + here
+    maps = [parts(got_ref[g, :, :n]) for g in range(fronts)]
+    gains = [got_ref[g, :, n : 2 * n] for g in range(fronts)]
+    joint = {g: parts(dot3(maps[g], maps[g + 1])) for g in range(1, fronts - 1, 2)}
+    ahead_v[0] = zero
+    ahead_v[1] = gains[0]
+    state = gains[0]
+    pushes = [None] * fronts
+
+    def push(g, pair):
+        pushes[g] = dot3(pair, parts(got_ref[g, :, 2 * n : 3 * n])) + got_ref[g, :, 3 * n :]
+
+    for g in range(1, fronts - 1, 2):
+        pair = parts(state)
+        state = dot3(pair, joint[g]) + (dot3(parts(gains[g]), maps[g + 1]) + gains[g + 1])
+        push(g, pair)
+        between = dot3(pair, maps[g]) + gains[g]
+        ahead_v[g + 1] = between
+        push(g + 1, parts(between))
+        ahead_v[g + 2] = state
+    push(fronts - 1, parts(state))
+    behind_v[fronts - 1] = zero
+    state = pushes[fronts - 1]
+    behind_v[fronts - 2] = state
+    for g in range(fronts - 3, 0, -2):
+        pair = parts(state)
+        state = dot3(pair, joint[g], NT) + (dot3(parts(pushes[g + 1]), maps[g], NT) + pushes[g])
+        behind_v[g] = dot3(pair, maps[g + 1], NT) + pushes[g + 1]
+        behind_v[g - 1] = state
 
     ahead = parts(ahead_v[mine])
     wave = wave_ref[...] + dot3(ahead, (wave_top[...], wave_rest[...]))
@@ -329,8 +369,8 @@
     ut = jnp.swapaxes(u_fac, 1, 2)
     vt = jnp.swapaxes(v_fac, 1, 2)
     cells = cellmap.reshape(-1, LANES)
-    live = jnp.clip(ranks[0] - jnp.arange(n, dtype=jnp.int32), 0, 1).astype(F32)
-    following = from_behind(vt[0] * live[:, None], "front", -1)
+    middle = np.repeat(np.arange(n, dtype=np.float32)[:, None] + 0.5, width, axis=1)
+    following = from_behind(jnp.where(middle < ranks[0].astype(F32), vt[0], 0.0), "front", -1)
 
     smem = pl.BlockSpec(memory_space=pltpu.SMEM)
     vmem = pl.BlockSpec(memory_space=pltpu.VMEM)
@@ -379,8 +419,7 @@
         in_specs=[vmem] * 4,
         out_specs=[vmem] * 2,
         cost_estimate=cost(0.5),
-        compiler_params=room,
-    )(*held(y, maps, following, back))
+            )(*held(y, maps, following, back))
 
     got = lax.all_to_all(send, "front", 0, 0)
 

time: 46.5 us -> 39.6 us (0.85)
  Pallas kernels: 23.6 us -> 16.7 us
  starting transfers between devices: 14.7 us -> 12.2 us
  waiting for transfers between devices: 4.29 us -> 6.73 us
  other arithmetic: 1.49 us -> 0.79 us
  between operations: 0.69 us -> 1.33 us
    pallas_call x1, Pallas kernels: 9.45 us -> 4.86 us  [body(): pl.pallas_call(prep_kernel, name='prep', out_shape=(pltpu.VMEM((blocks, s...]
    all_to_all x1, starting transfers between devices: 4.97 us -> 3.11 us  [body(): terms = lax.all_to_all(image, ('front', 'rhs'), 0, 0)]
    all_to_all x1, waiting for transfers between devices: 1.13 us -> 2.98 us  [body(): got = lax.all_to_all(send, 'front', 0, 0)]
    pallas_call x1, Pallas kernels: 6.21 us -> 4.35 us  [body(): pl.pallas_call(functools.partial(fields_kernel, fronts, slot), name='fiel...]
    mul x1 -> x0, other arithmetic: 0.83 us -> none  [body(): following = from_behind(vt[0] * live[:, None], 'front', -1)]
    select_n x0 -> x1, other arithmetic: none -> 0.79 us  [body(): jnp.where(middle < ranks[0].astype(F32), vt[0], 0.0)]
    convert_element_type x1 -> x0, other arithmetic: 0.65 us -> none  [body(): live = jnp.clip(ranks[0] - jnp.arange(n, dtype=jnp.int32), 0, 1).astype(F32)]
    ppermute x1, waiting for transfers between devices: 0.01 us -> 0.59 us  [from_behind(): return lax.ppermute(array, axis, pairs)]
  transfers between devices with their start and end apart: 3 -> 3, of which waited for: 2 -> 3; matrix products, arithmetic and copies ran while one was open for 3% -> 4% of each run, Pallas kernels for 40% -> 31%
where the time goes in v3:
time: 39.6 us; the launch traced here: 39.1 us
  Pallas kernels  16.7 us (42%)
  starting transfers between devices  12.2 us (31%)
  waiting for transfers between devices  6.73 us (17%)
  local copies, waits for them, and re-layouts  1.41 us (4%)
  between operations  1.33 us (3%)
  other arithmetic  0.79 us (2%)
    all_to_all x1, starting transfers between devices, body(): got = lax.all_to_all(send, 'front', 0, 0)  7.85 us
    pallas_call x1, Pallas kernels, body(): pl.pallas_call(prep_kernel, name='prep', out_shape=(pltpu.VMEM((blocks, s...  4.86 us
    pallas_call x1, Pallas kernels, body(): pl.pallas_call(functools.partial(fields_kernel, fronts, slot), name='fiel...  4.35 us
    all_to_all x1, waiting for transfers between devices, body(): terms = lax.all_to_all(image, ('front', 'rhs'), 0, 0)  3.15 us
    all_to_all x1, starting transfers between devices, body(): terms = lax.all_to_all(image, ('front', 'rhs'), 0, 0)  3.11 us
    all_to_all x1, waiting for transfers between devices, body(): got = lax.all_to_all(send, 'front', 0, 0)  2.98 us
    pallas_call x1, Pallas kernels, body(): pl.pallas_call(functools.partial(table_kernel, fronts, slot), name='table...  2.84 us
    pallas_call x1, Pallas kernels, body(): pl.pallas_call(functools.partial(solve_kernel, fronts, rhs), name='solve'...  2.51 us
  transfers between devices with their start and end apart: 3, of which 3 were waited for; matrix products, arithmetic and copies ran while one was open for 4% of the time, Pallas kernels for 31%

profile of v3, /device:TPU:0, one launch (start us, length us, event | category | flops | bytes accessed | tf_op | source)
XLA Modules:
  0.0 39.1 jit_solution(16951495505364055671)
XLA Ops:
  1.3 0.8 %fusion = f32[32,256]{1,0:T(8,128)S(1)} fusion(f32[8,32,256]{2,1,0:T(8,128)} %bitcast.11, f32[32,256]{1,0:T(8,128)} %constant.10.clone, f32[]{:T(128)} %bitcast.3), kind=kLoop, calls=%fused_computation.1 | loop fusion | flops 16384 | bytes 98308 | tf_op jit(solution)/shard_map/jit(_where)/select_n | solution.py:373
  2.1 1.3 %collective-permute-start = (f32[32,256]{1,0:T(8,128)S(1)}, f32[32,256]{1,0:T(8,128)S(1)}, u32[]{:S(2)}, u32[]{:S(2)}) collective-permute-start(f32[32,256]{1,0:T(8,128)S(1)} %fusion), channel_id=1, source_target_pairs={{4,0},{8,4},{12,8},{16,12},{20,16},{24,20},{28,24},{5,1},{9,5},{13... | collective-permute-start | bytes 98312 | tf_op jit(solution)/shard_map/ppermute | solution.py:49
  3.4 4.9 %prep.1 = (f32[8,64,256]{2,1,0:T(8,128)S(1)}, f32[8,64,128]{2,1,0:T(8,128)S(1)}, f32[64,32]{1,0:T(8,128)S(1)}) custom-call(s32[8]{0:T(128)} %ranks_hbm.3, s32[32,512]{1,0:T(8,128)} %signs_hbm.1, bf16[512,2048]{1,0:T(8,128)(2,1)} %sources_hbm.1, f32[8,256,256]{2,1,0:T(8,128)} %dinv_hbm.3, f32[8,32,256]{2,1,0:T(8,128)} %bitcast.14, f32[8,32,256]{2,1,0:T(8,128)} %bitcast.12, ...), custom_call_target="tpu_custom_call" | custom-call | flops 6000000000 | bytes 18000000 | tf_op jit(solution)/shard_map/prep/pallas_call | solution.py:390
  8.2 0.6 %collective-permute-done.next_ref = f32[32,256]{1,0:T(8,128)S(1)} collective-permute-done((f32[32,256]{1,0:T(8,128)S(1)}, f32[32,256]{1,0:T(8,128)S(1)}, u32[]{:S(2)}, u32[]{:S(2)}) %collective-permute-start) | collective-permute-done | bytes 32800 | tf_op jit(solution)/shard_map/ppermute | solution.py:49
  8.8 1.0 %send.1 = (f32[8,32,128]{2,1,0:T(8,128)}, f32[32,32]{1,0:T(8,128)S(1)}) custom-call(f32[8,64,256]{2,1,0:T(8,128)S(1)} %get-tuple-element.24.y_ref, f32[8,64,128]{2,1,0:T(8,128)S(1)} %get-tuple-element.25.maps_ref, f32[32,256]{1,0:T(8,128)S(1)} %collective-permute-done.next_ref, f32[64,32]{1,0:T(8,128)S(1)} %get-tuple-element.26.back_ref), custom_call_target="tpu_custom_call" | custom-call | flops 500000000 | bytes 1500000 | tf_op jit(solution)/shard_map/send/pallas_call | solution.py:415
  9.9 7.9 %all-to-all-start = ((f32[8,32,128]{2,1,0:T(8,128)}), f32[8,32,128]{2,1,0:T(8,128)S(1)}, u32[]{:S(2)}, u32[]{:S(2)}) async-start(f32[8,32,128]{2,1,0:T(8,128)} %get-tuple-element.27), calls=%async_computation | async-start | bytes 262144 | tf_op jit(solution)/shard_map/all_to_all | solution.py:424
  17.7 4.4 %fields.1 = (f32[32,2048]{1,0:T(8,128)S(1)}, bf16[32,2048]{1,0:T(8,128)(2,1)S(1)}, bf16[32,2048]{1,0:T(8,128)(2,1)S(1)}, f32[32,2048]{1,0:T(8,128)S(1)}, bf16[32...) custom-call(s32[1]{0:T(128)} %bitcast.front_ref, ...), custom_call_target="tpu_custom_call" | custom-call | flops 5000000000 | bytes 15000000 | tf_op jit(solution)/shard_map/fields/pallas_call | solution.py:426
  22.1 3.0 %all-to-all-done.got_ref = f32[8,32,128]{2,1,0:T(8,128)S(1)} async-done(((f32[8,32,128]{2,1,0:T(8,128)}), f32[8,32,128]{2,1,0:T(8,128)S(1)}, u32[]{:S(2)}, u32[]{:S(2)}) %all-to-all-start) | async-done | bytes 131104 | tf_op jit(solution)/shard_map/all_to_all | solution.py:424
  25.1 2.5 %solve.1 = (f32[32,2048]{1,0:T(8,128)S(1)}, f32[32,2048]{1,0:T(8,128)S(1)}, f32[32,4,128]{2,1,0:T(4,128)}, f32[8,128]{1,0:T(8,128)S(1)}) custom-call(s32[1]{0:T(128)} %bitcast.front_ref, f32[8,32,128]{2,1,0:T(8,128)S(1)} %all-to-all-done.got_ref, f32[32,2048]{1,0:T(8,128)S(1)} %get-tuple-element.29.wave_ref, ...), custom_call_target="tpu_custom_call" | custom-call | flops 3000000000 | bytes 9000000 | tf_op jit(solution)/shard_map/solve/pallas_call | solution.py:456
  27.6 3.1 %all-to-all-start.1 = ((f32[32,4,128]{2,1,0:T(4,128)}), f32[32,4,128]{2,1,0:T(4,128)S(1)}, u32[]{:S(2)}, u32[]{:S(2)}) async-start(f32[32,4,128]{2,1,0:T(4,128)} %get-tuple-element.41), calls=%async_computation.1 | async-start | bytes 131072 | tf_op jit(solution)/shard_map/all_to_all | solution.py:475
  30.7 2.8 %tables.1 = (bf16[64,4096]{1,0:T(8,128)(2,1)S(1)}, bf16[128,4096]{1,0:T(8,128)(2,1)S(1)}) custom-call(s32[1]{0:T(128)} %bitcast.front_ref, s32[128,128]{1,0:T(8,128)} %bitcast.16, f32[8,128]{1,0:T(8,128)S(1)} %get-tuple-element.42.token_ref), custom_call_target="tpu_custom_call" | custom-call | flops 4000000000 | bytes 12000000 | tf_op jit(solution)/shard_map/tables/pallas_call | solution.py:477
  33.5 0.7 %copy.12 = f32[32,2048]{1,0:T(8,128)} copy(f32[32,2048]{1,0:T(8,128)S(1)} %get-tuple-element.45) | data formatting | bytes 524288
  34.2 0.7 %copy.13 = f32[32,2048]{1,0:T(8,128)} copy(f32[32,2048]{1,0:T(8,128)S(1)} %get-tuple-element.46) | data formatting | bytes 524288
  34.9 3.2 %all-to-all-done.1.terms_ref = f32[32,4,128]{2,1,0:T(4,128)S(1)} async-done(((f32[32,4,128]{2,1,0:T(4,128)}), f32[32,4,128]{2,1,0:T(4,128)S(1)}, u32[]{:S(2)}, u32[]{:S(2)}) %all-to-all-start.1) | async-done | bytes 65568 | tf_op jit(solution)/shard_map/all_to_all | solution.py:475
  38.1 1.1 %gather.1 = f32[64,128]{1,0:T(8,128)} custom-call(f32[32,4,128]{2,1,0:T(4,128)S(1)} %all-to-all-done.1.terms_ref, bf16[64,4096]{1,0:T(8,128)(2,1)S(1)} %get-tuple-element.43.hit_ref, bf16[128,4096]{1,0:T(8,128)(2,1)S(1)} %get-tuple-element.44.pick_ref), custom_call_target="tpu_custom_call" | custom-call | flops 1000000000 | bytes 3000000 | tf_op jit(solution)/shard_map/gather/pallas_call | solution.py:490
Async XLA Ops:
  2.1 6.7 %collective-permute-start = (f32[32,256]{1,0:T(8,128)S(1)}, f32[32,256]{1,0:T(8,128)S(1)}, u32[]{:S(2)}, u32[]{:S(2)}) collective-permute-start(f32[32,256]{1,0:T(8,128)S(1)} %fusion), channel_id=1, source_target_pairs={{4,0},{8,4},{12,8},{16,12},{20,16},{24,20},{28,24},{5,1},{9,5},{13... | collective-permute-start | bytes 98312 | tf_op jit(solution)/shard_map/ppermute | solution.py:49
  9.9 15.2 %all-to-all-start = ((f32[8,32,128]{2,1,0:T(8,128)}), f32[8,32,128]{2,1,0:T(8,128)S(1)}, u32[]{:S(2)}, u32[]{:S(2)}) async-start(f32[8,32,128]{2,1,0:T(8,128)} %get-tuple-element.27), calls=%async_computation | async-start | bytes 262144 | tf_op jit(solution)/shard_map/all_to_all | solution.py:424
  27.6 10.5 %all-to-all-start.1 = ((f32[32,4,128]{2,1,0:T(4,128)}), f32[32,4,128]{2,1,0:T(4,128)S(1)}, u32[]{:S(2)}, u32[]{:S(2)}) async-start(f32[32,4,128]{2,1,0:T(4,128)} %get-tuple-element.41), calls=%async_computation.1 | async-start | bytes 131072 | tf_op jit(solution)/shard_map/all_to_all | solution.py:475

commit v4 on v3

--- a/solution.py
+++ b/solution.py
@@ -45,8 +45,7 @@
 
 def from_behind(array, axis, by):
     length = lax.axis_size(axis)
-    pairs = [(i, i + by) for i in range(length) if 0 <= i + by < length]
-    return lax.ppermute(array, axis, pairs)
+    return lax.ppermute(array, axis, [(i, (i + by) % length) for i in range(length)])
 
 
 def prep_kernel(
@@ -110,35 +109,37 @@
 
     n = rank_max
     nothing = jnp.zeros((n, n), F32)
-
-    def follow(span, k):
-        later = dot3(span, parts(steps[k][shots:]))
-        return jnp.concatenate([later[:shots] + steps[k][:shots], later[shots:]], axis=0)
-
-    steps = [jnp.concatenate([seen[:shots, :n], -seen[2 * shots :, :n]], axis=0) for seen in map(products.get, range(blocks))]
-    joint = {k: follow(parts(steps[k]), k + 1) for k in range(1, blocks - 2, 2)}
-    spans = [steps[0]]
-    for k in range(1, blocks - 1, 2):
-        pair = parts(spans[-1])
-        spans.append(follow(pair, k))
+    gains = [products[k][:shots, :n] for k in range(blocks)]
+    fills = [products[k][shots : 2 * shots, n:] for k in range(blocks)]
+    boths = [products[k][2 * shots :] for k in range(blocks)]
+
+    def over(upper, product):
+        return jnp.concatenate([upper - product[:shots], -product[shots:]], axis=0)
+
+    joint = {}
+    for k in range(1, blocks - 2, 2):
+        follow = jnp.concatenate([gains[k], -boths[k][:, :n]], axis=0)
+        joint[k] = over(gains[k + 1], dot3(parts(follow), parts(boths[k + 1][:, :n])))
+    states = [None] * blocks
+    states[1] = jnp.concatenate([gains[0], -boths[0][:, :n]], axis=0)
+    pushes = [jnp.concatenate([fills[0], -boths[0][:, n:]], axis=0)] + [None] * (blocks - 1)
+    for k in range(1, blocks):
+        weights = [boths[k]]
         if k in joint:
-            later = dot3(pair, parts(joint[k][shots:]))
-            spans.append(jnp.concatenate([later[:shots] + joint[k][:shots], later[shots:]], axis=0))
-    back = None
+            weights.append(-joint[k][shots:])
+        after = dot3(parts(states[k]), parts(jnp.concatenate(weights, axis=1)))
+        pushes[k] = over(fills[k], after[:, n : 2 * n])
+        if k % 2 and k + 1 < blocks:
+            states[k + 1] = over(gains[k], after[:, :n])
+        if k in joint:
+            states[k + 2] = over(joint[k][:shots], after[:, 2 * n :])
+    long = jnp.concatenate(pushes[1:], axis=1)
+    back = pushes[0] + dot3(parts(long), parts(jnp.concatenate([state[shots:] for state in states[1:]], axis=1)), NT)
     for k in range(blocks):
-        seen = products[k]
-        push = jnp.concatenate([seen[shots : 2 * shots, n:], nothing], axis=0)
-        if k == 0:
-            push = push - jnp.concatenate([nothing, seen[2 * shots :, n:]], axis=0)
-            back = push
-        else:
-            pair = parts(spans[k - 1])
-            push = push - dot3(pair, parts(seen[2 * shots :, n:]))
-            back = back + dot3(parts(push), rows_of(pair, shots, None), NT)
         if k + 1 < blocks:
-            maps_ref[k, :, :n] = spans[k]
-        maps_ref[k, :, n : 2 * n] = push
-        maps_ref[k, :n, 2 * n :] = seen[2 * shots :]
+            maps_ref[k, :, :n] = states[k + 1]
+        maps_ref[k, :, n : 2 * n] = pushes[k]
+        maps_ref[k, :n, 2 * n :] = boths[k]
     back_ref[...] = back
 
 
@@ -159,13 +160,14 @@
 
 def fields_kernel(
     fronts, slot, front_ref, y_ref, maps_ref, next_ref, last_ref, map_hbm, dinv_hbm, vt_hbm, dobs_hbm, ranks_hbm,
-    wave_ref, wave_top, wave_rest, adj_ref, ahead_top, ahead_rest, behind_top, behind_rest, hit_ref, pick_ref,
+    wave_ref, wave_top, wave_rest, adj_ref, ahead_top, ahead_rest, behind_top, behind_rest, hit_ref, pick_ref, mine_ref,
     map_v, dinv_v, vt_v, dobs_v, ranks_ref, sem, block_sem,
 ):
     blocks, n, width = vt_v.shape
     shots = dobs_v.shape[0]
     groups = map_v.shape[0]
     start = pl.multiple_of(front_ref[0] * groups, groups)
+    mine_ref[...] = (lax.broadcasted_iota(jnp.int32, mine_ref.shape, 0) == front_ref[0]).astype(F32)
     fetch = [
         pltpu.make_async_copy(vt_hbm, vt_v, sem.at[0]),
         pltpu.make_async_copy(dobs_hbm, dobs_v, sem.at[1]),
@@ -250,15 +252,14 @@
 
 
 def solve_kernel(
-    fronts, rhs, front_ref, got_ref, wave_ref, wave_top, wave_rest, adj_ref, ahead_top, ahead_rest,
-    behind_top, behind_rest, hit_ref, pick_ref,
+    fronts, rhs, got_ref, wave_ref, wave_top, wave_rest, adj_ref, ahead_top, ahead_rest,
+    behind_top, behind_rest, hit_ref, pick_ref, mine_ref,
     wave_out, adj_out, image_out, token_ref,
-    ahead_v, behind_v,
 ):
     shots, rows = wave_ref.shape
     n = wave_top.shape[0]
-    mine = front_ref[0]
     token_ref[...] = jnp.zeros_like(token_ref)
+    ahead_v, behind_v = {}, {}
     zero = jnp.zeros((shots, n), F32)
 
     maps = [parts(got_ref[g, :, :n]) for g in range(fronts)]
@@ -290,11 +291,17 @@
         behind_v[g] = dot3(pair, maps[g + 1], NT) + pushes[g + 1]
         behind_v[g - 1] = state
 
-    ahead = parts(ahead_v[mine])
+    def own(choices):
+        value = choices[0]
+        for g in range(1, fronts):
+            value = jnp.where(mine_ref[g : g + 1, :n] > 0.5, choices[g], value)
+        return parts(value)
+
+    ahead = own(ahead_v)
     wave = wave_ref[...] + dot3(ahead, (wave_top[...], wave_rest[...]))
     wave_out[...] = wave
     adj = adj_ref[...] + dot3(ahead, (ahead_top[...], ahead_rest[...]))
-    adj = adj + dot3(parts(behind_v[mine]), (behind_top[...], behind_rest[...]))
+    adj = adj + dot3(own(behind_v), (behind_top[...], behind_rest[...]))
     adj_out[...] = adj
     image = jnp.sum(wave * adj, axis=0, keepdims=True) * (1.0 / (shots * rhs))
     top, rest = parts(image)
@@ -370,7 +377,8 @@
     vt = jnp.swapaxes(v_fac, 1, 2)
     cells = cellmap.reshape(-1, LANES)
     middle = np.repeat(np.arange(n, dtype=np.float32)[:, None] + 0.5, width, axis=1)
-    following = from_behind(jnp.where(middle < ranks[0].astype(F32), vt[0], 0.0), "front", -1)
+    alive = jnp.where(lax.axis_index("front") == 0, 0, ranks[0]).astype(F32)
+    following = from_behind(jnp.where(middle < alive, vt[0], 0.0), "front", -1)
 
     smem = pl.BlockSpec(memory_space=pltpu.SMEM)
     vmem = pl.BlockSpec(memory_space=pltpu.VMEM)
@@ -437,9 +445,10 @@
             pltpu.VMEM((n, rows), BF16),
             pltpu.VMEM((fronts * each, rows), BF16),
             pltpu.VMEM((LANES, rows), BF16),
+            pltpu.VMEM((fronts, LANES), F32),
         ),
         in_specs=[smem] + [vmem] * 4 + [hbm] * 5,
-        out_specs=[vmem] * 10,
+        out_specs=[vmem] * 11,
         scratch_shapes=[
             pltpu.VMEM((groups, LANES), cells.dtype),
             pltpu.VMEM(dinv.shape, dinv.dtype),
@@ -462,15 +471,11 @@
             pltpu.VMEM((fronts * rhs, each, LANES), F32),
             pltpu.VMEM((8, LANES), F32),
         ),
-        in_specs=[smem] + [vmem] * 11,
+        in_specs=[vmem] * 12,
         out_specs=[vmem] * 4,
-        scratch_shapes=[
-            pltpu.VMEM((fronts, shots, n), F32),
-            pltpu.VMEM((fronts, shots, n), F32),
-        ],
         cost_estimate=cost(3),
         compiler_params=room,
-    )(front, *held(got, *fields))
+    )(*held(got, *fields))
 
     terms = lax.all_to_all(image, ("front", "rhs"), 0, 0)
 

time: 39.6 us -> 39.2 us (0.990)
  waiting for transfers between devices: 6.73 us -> 6.07 us
    ppermute x1, starting transfers between devices: 1.28 us -> 6 us  [from_behind(): lax.ppermute(array, axis, [(i, (i + by) % length) for i in range(length)])]
    all_to_all x1, starting transfers between devices: 7.85 us -> 3.37 us  [body(): got = lax.all_to_all(send, 'front', 0, 0)]
    ppermute x1, waiting for transfers between devices: 0.59 us -> 0.01 us  [from_behind(): lax.ppermute(array, axis, [(i, (i + by) % length) for i in range(length)])]
  transfers between devices with their start and end apart: 3 -> 3, of which waited for: 3 -> 2; matrix products, arithmetic and copies ran while one was open for 4% -> 4% of each run, Pallas kernels for 31% -> 31%
where the time goes in v4:
time: 39.2 us; the launch traced here: 38.8 us
  Pallas kernels  16.7 us (43%)
  starting transfers between devices  12.5 us (32%)
  waiting for transfers between devices  6.07 us (15%)
  local copies, waits for them, and re-layouts  1.41 us (4%)
  between operations  1.34 us (3%)
  other arithmetic  0.79 us (2%)
    ppermute x1, starting transfers between devices, from_behind(): lax.ppermute(array, axis, [(i, (i + by) % length) for i in range(length)])  6 us
    pallas_call x1, Pallas kernels, body(): pl.pallas_call(prep_kernel, name='prep', out_shape=(pltpu.VMEM((blocks, s...  4.9 us
    pallas_call x1, Pallas kernels, body(): pl.pallas_call(functools.partial(fields_kernel, fronts, slot), name='fiel...  4.36 us
    all_to_all x1, starting transfers between devices, body(): got = lax.all_to_all(send, 'front', 0, 0)  3.37 us
    all_to_all x1, waiting for transfers between devices, body(): terms = lax.all_to_all(image, ('front', 'rhs'), 0, 0)  3.15 us
    all_to_all x1, starting transfers between devices, body(): terms = lax.all_to_all(image, ('front', 'rhs'), 0, 0)  3.11 us
    all_to_all x1, waiting for transfers between devices, body(): got = lax.all_to_all(send, 'front', 0, 0)  2.91 us
    pallas_call x1, Pallas kernels, body(): pl.pallas_call(functools.partial(table_kernel, fronts, slot), name='table...  2.84 us
  transfers between devices with their start and end apart: 3, of which 2 were waited for; matrix products, arithmetic and copies ran while one was open for 4% of the time, Pallas kernels for 31%

profile of v4, /device:TPU:0, one launch (start us, length us, event | category | flops | bytes accessed | tf_op | source)
XLA Modules:
  0.0 38.8 jit_solution(2930246619351121405)
XLA Ops:
  1.3 0.8 %fusion = f32[32,256]{1,0:T(8,128)S(1)} fusion(f32[8,32,256]{2,1,0:T(8,128)} %bitcast.11, f32[32,256]{1,0:T(8,128)} %constant.12.clone, f32[]{:T(128)S(6)} %convert_element_type.3), kind=kLoop, calls=%fused_computation.1 | loop fusion | flops 16384 | bytes 98308 | tf_op jit(solution)/shard_map/jit(_where)/select_n | solution.py:381
  2.1 6.0 %collective-permute-start = (f32[32,256]{1,0:T(8,128)S(1)}, f32[32,256]{1,0:T(8,128)S(1)}, u32[]{:S(2)}, u32[]{:S(2)}) collective-permute-start(f32[32,256]{1,0:T(8,128)S(1)} %fusion), channel_id=1, source_target_pairs={{0,28},{4,0},{8,4},{12,8},{16,12},{20,16},{24,20},{28,24},{1,29},{... | collective-permute-start | bytes 98312 | tf_op jit(solution)/shard_map/ppermute | solution.py:48
  8.1 4.9 %prep.1 = (f32[8,64,256]{2,1,0:T(8,128)S(1)}, f32[8,64,128]{2,1,0:T(8,128)S(1)}, f32[64,32]{1,0:T(8,128)S(1)}) custom-call(s32[8]{0:T(128)} %ranks_hbm.3, s32[32,512]{1,0:T(8,128)} %signs_hbm.1, bf16[512,2048]{1,0:T(8,128)(2,1)} %sources_hbm.1, f32[8,256,256]{2,1,0:T(8,128)} %dinv_hbm.3, f32[8,32,256]{2,1,0:T(8,128)} %bitcast.15, f32[8,32,256]{2,1,0:T(8,128)} %bitcast.12, ...), custom_call_target="tpu_custom_call" | custom-call | flops 6000000000 | bytes 18000000 | tf_op jit(solution)/shard_map/prep/pallas_call | solution.py:398
  13.0 0.0 collective-permute-done.next_ref
  13.0 1.0 %send.1 = (f32[8,32,128]{2,1,0:T(8,128)}, f32[32,32]{1,0:T(8,128)S(1)}) custom-call(f32[8,64,256]{2,1,0:T(8,128)S(1)} %get-tuple-element.25.y_ref, f32[8,64,128]{2,1,0:T(8,128)S(1)} %get-tuple-element.26.maps_ref, f32[32,256]{1,0:T(8,128)S(1)} %collective-permute-done.next_ref, f32[64,32]{1,0:T(8,128)S(1)} %get-tuple-element.27.back_ref), custom_call_target="tpu_custom_call" | custom-call | flops 500000000 | bytes 1500000 | tf_op jit(solution)/shard_map/send/pallas_call | solution.py:423
  14.0 3.4 %all-to-all-start = ((f32[8,32,128]{2,1,0:T(8,128)}), f32[8,32,128]{2,1,0:T(8,128)S(1)}, u32[]{:S(2)}, u32[]{:S(2)}) async-start(f32[8,32,128]{2,1,0:T(8,128)} %get-tuple-element.28), calls=%async_computation | async-start | bytes 262144 | tf_op jit(solution)/shard_map/all_to_all | solution.py:432
  17.4 4.4 %fields.1 = (f32[32,2048]{1,0:T(8,128)S(1)}, bf16[32,2048]{1,0:T(8,128)(2,1)S(1)}, bf16[32,2048]{1,0:T(8,128)(2,1)S(1)}, f32[32,2048]{1,0:T(8,128)S(1)}, bf16[32...) custom-call(s32[1]{0:T(128)} %bitcast.4.front_ref, ...), custom_call_target="tpu_custom_call" | custom-call | flops 5000000000 | bytes 15000000 | tf_op jit(solution)/shard_map/fields/pallas_call | solution.py:434
  21.8 2.9 %all-to-all-done.got_ref = f32[8,32,128]{2,1,0:T(8,128)S(1)} async-done(((f32[8,32,128]{2,1,0:T(8,128)}), f32[8,32,128]{2,1,0:T(8,128)S(1)}, u32[]{:S(2)}, u32[]{:S(2)}) %all-to-all-start) | async-done | bytes 131104 | tf_op jit(solution)/shard_map/all_to_all | solution.py:432
  24.7 2.5 %solve.1 = (f32[32,2048]{1,0:T(8,128)S(1)}, f32[32,2048]{1,0:T(8,128)S(1)}, f32[32,4,128]{2,1,0:T(4,128)}, f32[8,128]{1,0:T(8,128)S(1)}) custom-call(f32[8,32,128]{2,1,0:T(8,128)S(1)} %all-to-all-done.got_ref, f32[32,2048]{1,0:T(8,128)S(1)} %get-tuple-element.30.wave_ref, bf16[32,2048]{1,0:T(8,128)(2,1)S(1)} %get-tuple-element.31.wave_top, ...), custom_call_target="tpu_custom_call" | custom-call | flops 3000000000 | bytes 9000000 | tf_op jit(solution)/shard_map/solve/pallas_call | solution.py:465
  27.2 3.1 %all-to-all-start.1 = ((f32[32,4,128]{2,1,0:T(4,128)}), f32[32,4,128]{2,1,0:T(4,128)S(1)}, u32[]{:S(2)}, u32[]{:S(2)}) async-start(f32[32,4,128]{2,1,0:T(4,128)} %get-tuple-element.43), calls=%async_computation.1 | async-start | bytes 131072 | tf_op jit(solution)/shard_map/all_to_all | solution.py:480
  30.3 2.8 %tables.1 = (bf16[64,4096]{1,0:T(8,128)(2,1)S(1)}, bf16[128,4096]{1,0:T(8,128)(2,1)S(1)}) custom-call(s32[1]{0:T(128)} %bitcast.4.front_ref, s32[128,128]{1,0:T(8,128)} %bitcast.17, f32[8,128]{1,0:T(8,128)S(1)} %get-tuple-element.44.token_ref), custom_call_target="tpu_custom_call" | custom-call | flops 4000000000 | bytes 12000000 | tf_op jit(solution)/shard_map/tables/pallas_call | solution.py:482
  33.2 0.7 %copy.12 = f32[32,2048]{1,0:T(8,128)} copy(f32[32,2048]{1,0:T(8,128)S(1)} %get-tuple-element.47) | data formatting | bytes 524288
  33.9 0.7 %copy.13 = f32[32,2048]{1,0:T(8,128)} copy(f32[32,2048]{1,0:T(8,128)S(1)} %get-tuple-element.48) | data formatting | bytes 524288
  34.6 3.2 %all-to-all-done.1.terms_ref = f32[32,4,128]{2,1,0:T(4,128)S(1)} async-done(((f32[32,4,128]{2,1,0:T(4,128)}), f32[32,4,128]{2,1,0:T(4,128)S(1)}, u32[]{:S(2)}, u32[]{:S(2)}) %all-to-all-start.1) | async-done | bytes 65568 | tf_op jit(solution)/shard_map/all_to_all | solution.py:480
  37.7 1.1 %gather.1 = f32[64,128]{1,0:T(8,128)} custom-call(f32[32,4,128]{2,1,0:T(4,128)S(1)} %all-to-all-done.1.terms_ref, bf16[64,4096]{1,0:T(8,128)(2,1)S(1)} %get-tuple-element.45.hit_ref, bf16[128,4096]{1,0:T(8,128)(2,1)S(1)} %get-tuple-element.46.pick_ref), custom_call_target="tpu_custom_call" | custom-call | flops 1000000000 | bytes 3000000 | tf_op jit(solution)/shard_map/gather/pallas_call | solution.py:495
Async XLA Ops:
  2.1 10.9 %collective-permute-start = (f32[32,256]{1,0:T(8,128)S(1)}, f32[32,256]{1,0:T(8,128)S(1)}, u32[]{:S(2)}, u32[]{:S(2)}) collective-permute-start(f32[32,256]{1,0:T(8,128)S(1)} %fusion), channel_id=1, source_target_pairs={{0,28},{4,0},{8,4},{12,8},{16,12},{20,16},{24,20},{28,24},{1,29},{... | collective-permute-start | bytes 98312 | tf_op jit(solution)/shard_map/ppermute | solution.py:48
  14.0 10.7 %all-to-all-start = ((f32[8,32,128]{2,1,0:T(8,128)}), f32[8,32,128]{2,1,0:T(8,128)S(1)}, u32[]{:S(2)}, u32[]{:S(2)}) async-start(f32[8,32,128]{2,1,0:T(8,128)} %get-tuple-element.28), calls=%async_computation | async-start | bytes 262144 | tf_op jit(solution)/shard_map/all_to_all | solution.py:432
  27.2 10.5 %all-to-all-start.1 = ((f32[32,4,128]{2,1,0:T(4,128)}), f32[32,4,128]{2,1,0:T(4,128)S(1)}, u32[]{:S(2)}, u32[]{:S(2)}) async-start(f32[32,4,128]{2,1,0:T(4,128)} %get-tuple-element.43), calls=%async_computation.1 | async-start | bytes 131072 | tf_op jit(solution)/shard_map/all_to_all | solution.py:480
